TPU v7x, 128 devices: a whole 4x4x4 slice. The times are simulated.
128 devices in a mesh: pairs: 32 (over y, z, core), items: 4 (over x).
Axes of the slice: x: 4, y: 4, z: 4, core: 2. Of those that a mesh axis runs over, the one named last changes fastest.
Arguments:
- user_table: bfloat16 [131072, 1024], P(('pairs', 'items'))
- item_table: bfloat16 [8192, 1024], P('items')
- pair_user: int32 [262144], P(('pairs', 'items')), may hold values from 0 to 1023
- pair_item: int32 [262144], P(('pairs', 'items')), may hold values from 0 to 2047
- pair_owner: int32 [262144], P(('pairs', 'items')), may hold values from 0 to 3, as said below
- pair_count: int32 [128], P(('pairs', 'items')), may hold values from 1024 to 2048, as said below
Outputs:
- r_user: float32 [1024, 1024], replicated
- r_item: float32 [1024, 1024], replicated
- whitened: float32 [1024, 1024], P(('pairs', 'items'))
Inputs may be any that keep to these rules, and one draw needn't show every extreme that they name: `pair_owner`: among the 2048 pair slots of one device at most 1024 name one owner; in every group of devices along items one owner is named by exactly 1024 slots of every device of the group. `pair_count`: some device has all 2048 slots valid.
All inputs are finite; a program needn't handle non-finite values.
Results may differ from a plain program's by a relative error of at most 0.0003.
Values may be sent and summed in bfloat16 or wider, within the bound.
No kernel may reach another device: no remote copies, remote signals or barrier semaphores. Data moves between devices by JAX's collectives and lax.ppermute only.
A program may use at most 128 MiB of HBM per device.

v0:
```python
import functools

import jax
import jax.numpy as jnp
from jax import lax
from jax.experimental import pallas as pl
from jax.experimental.pallas import tpu as pltpu
from jax.sharding import Mesh, PartitionSpec as P


N = 1024
NB = 128
KB = N // NB
SUB = 32
CHUNK = 512
SLOTS = 1024
HI = lax.Precision.HIGHEST
F32 = jnp.float32
BF16 = jnp.bfloat16
PACKED = 36 * NB
ALL = ("y", "z", "core", "x")
PAIRS_OF = [(i, j) for i in range(KB) for j in range(i, KB)]
START = {ij: NB * n for n, ij in enumerate(PAIRS_OF)}


def row_of(v, t):
    return jnp.broadcast_to(v[t:t + 1, :], v.shape)


def lane_of(v, c):
    return jnp.broadcast_to(v[:, c:c + 1], (8, NB))


def dot(a, b, ca, cb):
    return lax.dot_general(a, b, (((ca,), (cb,)), ((), ())), precision=HI, preferred_element_type=F32)


def parts(a):
    h = a.astype(BF16)
    rest = a - h.astype(F32)
    m = rest.astype(BF16)
    return h, m, (rest - m.astype(F32)).astype(BF16)


def stacks(a):
    h, m, l = parts(a)
    return jnp.concatenate([h, h, m, m, h, l], 0), jnp.concatenate([h, m, h, m, l, h], 0)


def tdot(a, b):
    return lax.dot_general(a, b, (((0,), (0,)), ((), ())), preferred_element_type=F32)


def factor(a, tmp):
    sub = lax.broadcasted_iota(jnp.int32, (8, NB), 0)
    groups = SUB // 8
    for s in range(NB // SUB):
        lo = SUB * s
        left = [a[lo + 8 * g:lo + 8 * g + 8, :NB] for g in range(groups)]
        right = [a[lo + 8 * g:lo + 8 * g + 8, NB:] for g in range(groups)]
        for g in range(groups):
            base = lo + 8 * g
            cols = [lane_of(left[g], base + t) for t in range(8)]
            for t in range(8):
                tmp[8 * t:8 * t + 8, :] = cols[t]
            ent = {(u, t): tmp[pl.ds(8 * t + u, 8, stride=0), :] for t in range(8) for u in range(t, 8)}
            fac, inv = {}, []
            for t in range(8):
                ri = lax.rsqrt(ent[t, t])
                inv.append(ri)
                for u in range(t + 1, 8):
                    fac[t, u] = ent[u, t] * ri
                for v in range(t + 1, 8):
                    for u in range(v, 8):
                        ent[u, v] = ent[u, v] - fac[t, u] * fac[t, v]
            rows_l, rows_r = [], []
            for t in range(8):
                pl_, pr_ = row_of(left[g], t), row_of(right[g], t)
                for k in range(t):
                    pl_ = pl_ - fac[k, t] * rows_l[k]
                    pr_ = pr_ - fac[k, t] * rows_r[k]
                rows_l.append(pl_ * inv[t])
                rows_r.append(pr_ * inv[t])
            for h in range(g + 1, groups):
                hc = [lane_of(left[h], base + t) for t in range(8)]
                for t in range(8):
                    ht = hc[t] * inv[t]
                    for u in range(t + 1, 8):
                        hc[u] = hc[u] - ht * fac[t, u]
                    left[h] = left[h] - ht * rows_l[t]
                    right[h] = right[h] - ht * rows_r[t]
            out_l, out_r = rows_l[0], rows_r[0]
            for t in range(1, 8):
                out_l = jnp.where(sub == t, rows_l[t], out_l)
                out_r = jnp.where(sub == t, rows_r[t], out_r)
            a[base:base + 8, :NB] = out_l
            a[base:base + 8, NB:] = out_r
        hi = lo + SUB
        if hi < NB:
            got = a[lo:hi, :]
            sa, sb = stacks(got)
            a[hi:, :] = a[hi:, :] - tdot(sa[:, hi:NB], sb)


def chol_kernel(scale, g_ref, out_ref, gp, r, a, tmp, got):
    row = lax.broadcasted_iota(jnp.int32, (NB, NB), 0)
    col = lax.broadcasted_iota(jnp.int32, (NB, NB), 1)
    eye = (row == col).astype(F32)

    def fetch(i):
        rows = pl.ds(START[i, i], NB * (KB - i))
        return pltpu.make_async_copy(g_ref.at[rows, :], gp.at[rows, :], got.at[i])

    for i in range(KB):
        fetch(i).start()
    for i in range(KB):
        fetch(i).wait()
        for j in range(i, KB):
            r[NB * i:NB * (i + 1), NB * j:NB * (j + 1)] = gp[START[i, j]:START[i, j] + NB, :] * scale

    def step(k, _):
        at = pl.multiple_of(k * NB, NB)
        here = pl.ds(at, NB)
        a[:, :NB] = r[here, here]
        a[:, NB:] = eye
        factor(a, tmp)
        out_ref[pl.ds(PACKED + at, NB), :] = a[:, NB:]
        r[here, here] = jnp.where(col >= row, a[:, :NB], 0.0)
        for s in range(KB - 1):
            @pl.when(k == s)
            def _(s=s):
                lo = NB * (s + 1)
                panel = dot(a[:, NB:], r[NB * s:lo, lo:], 1, 0)
                r[NB * s:lo, lo:] = panel
                sa, sb = stacks(panel)
                for i in range(lo, N, 256):
                    n = min(256, N - i)
                    r[i:i + n, i:] = r[i:i + n, i:] - tdot(sa[:, i - lo:i - lo + n], sb[:, i - lo:])
        return 0

    lax.fori_loop(0, KB, step, 0)
    for i, j in PAIRS_OF:
        out_ref[START[i, j]:START[i, j] + NB, :] = r[NB * i:NB * (i + 1), NB * j:NB * (j + 1)]


VM = pl.BlockSpec(memory_space=pltpu.VMEM)
HBM = pl.BlockSpec(memory_space=pltpu.HBM)
SM = pl.BlockSpec(memory_space=pltpu.SMEM)
PARAMS = pltpu.CompilerParams(vmem_limit_bytes=28 << 20)


def chol(packed, scale):
    return pl.pallas_call(
        functools.partial(chol_kernel, scale),
        out_shape=jax.ShapeDtypeStruct((PACKED + N, NB), F32),
        in_specs=[HBM],
        out_specs=VM,
        scratch_shapes=[
            pltpu.VMEM((PACKED, NB), F32),
            pltpu.VMEM((N, N), F32),
            pltpu.VMEM((NB, 2 * NB), F32),
            pltpu.VMEM((8 * 8, NB), F32),
            pltpu.SemaphoreType.DMA((KB,)),
        ],
        compiler_params=PARAMS,
        cost_estimate=pl.CostEstimate(flops=1 << 33, bytes_accessed=8 << 20, transcendentals=0),
        name="chol",
    )(packed)


def place(m):
    core, chip, x = m // 64, m // 4 % 16, m % 4
    return (chip * 2 + core) * 4 + x


def thin_kernel(core_ref, y_ref, mine_ref, other_ref, r_ref, out_ref, rp, r, w, y, got, left, *, maker, scale):
    def rows(k):
        return pl.ds(START[k, k], NB * (KB - k))

    def fetch(src, k):
        return pltpu.make_async_copy(src.at[rows(k), :], rp.at[rows(k), :], got.at[k])

    def inverses(src):
        return pltpu.make_async_copy(src.at[pl.ds(PACKED, N), :], w, got.at[KB])

    def leave(k):
        block = pl.ds(k * NB, NB)
        return pltpu.make_async_copy(r.at[block, :], r_ref.at[block, :], left.at[k])

    def load(src):
        inverses(src).start()
        for k in range(KB):
            fetch(src, k).start()

    pl.when(core_ref[0] == maker)(lambda: load(mine_ref))
    pl.when(core_ref[0] != maker)(lambda: load(other_ref))
    if maker:
        for k in range(KB):
            y[:, NB * k:NB * (k + 1)] = jnp.transpose(y_ref[NB * k:NB * (k + 1), :])[:8, :]
    else:
        y[...] = y_ref[...] * scale
    inverses(mine_ref).wait()
    for k in range(KB):
        lo, hi = k * NB, (k + 1) * NB
        yk = dot(y[:, lo:hi], w[lo:hi, :], 1, 1)
        if maker:
            out_ref[:, lo:hi] = yk
        else:
            for m in range(128):
                at = place(m) * 8 - lo
                if 0 <= at < NB:
                    out_ref[m, :, :] = pltpu.roll(yk, (NB - at) % NB, 1) if at else yk
        fetch(mine_ref, k).wait()
        blocks = [rp[START[k, j]:START[k, j] + NB, :] for j in range(k, KB)]
        if hi < N:
            y[:, hi:] = y[:, hi:] - dot(yk, jnp.concatenate(blocks[1:], 1), 1, 0)
            r[hi:, lo:hi] = jnp.zeros((N - hi, NB), F32)
        for j in range(k, KB):
            r[lo:hi, NB * j:NB * (j + 1)] = blocks[j - k]
        leave(k).start()
    for k in range(KB):
        leave(k).wait()


def thin(core, y, mine, other, maker, scale=1.0):
    out = (8, N) if maker else (128, 8, NB)
    return pl.pallas_call(
        functools.partial(thin_kernel, maker=maker, scale=scale),
        out_shape=(jax.ShapeDtypeStruct((N, N), F32), jax.ShapeDtypeStruct(out, F32)),
        in_specs=[SM, VM, HBM, HBM],
        out_specs=(HBM, VM),
        scratch_shapes=[
            pltpu.VMEM((PACKED, NB), F32),
            pltpu.VMEM((N, N), F32),
            pltpu.VMEM((N, NB), F32),
            pltpu.VMEM((8, N), F32),
            pltpu.SemaphoreType.DMA((KB + 1,)),
            pltpu.SemaphoreType.DMA((KB,)),
        ],
        compiler_params=pltpu.CompilerParams(vmem_limit_bytes=60 << 20),
        name="thin",
    )(core, y, mine, other)


def gram_kernel(core_ref, cu_ref, ci_ref, u_ref, i_ref, keep_ref, give_ref, counts, acc):
    eye = lax.broadcasted_iota(jnp.int32, (NB, NB), 0) == lax.broadcasted_iota(jnp.int32, (NB, NB), 1)

    def put(ref):
        for i, j in PAIRS_OF:
            at = START[i, j]
            ref[at:at + NB, :] = acc[NB * i:NB * (i + 1), NB * j:NB * (j + 1)]

    for maker, table in enumerate((u_ref, i_ref)):
        rows = table.shape[0]
        counts[:rows // NB, :] = ci_ref[...] if maker else cu_ref[...]
        acc[...] = jnp.zeros((N, N), F32)

        def chunk(c):
            times = [jnp.sum(jnp.where(eye, counts[pl.ds(c * (CHUNK // NB) + b, 1), :], 0.0), axis=1, keepdims=True) for b in range(CHUNK // NB)]
            t = table[pl.ds(pl.multiple_of(c * CHUNK, CHUNK), CHUNK), :]
            weighted = t.astype(F32) * jnp.concatenate(times, 0)
            high = weighted.astype(BF16)
            both = jnp.concatenate([high, (weighted - high.astype(F32)).astype(BF16)], 0)
            tt = jnp.concatenate([t, t], 0)
            for i in range(0, N, 256):
                acc[i:i + 256, i:] = acc[i:i + 256, i:] + tdot(tt[:, i:i + 256], both[:, i:])

        def chunks(c, _):
            for k in range(1 + maker):
                chunk(c * (1 + maker) + k)
            return 0

        lax.fori_loop(0, 2, chunks, 0)
        pl.when(core_ref[0] == maker)(lambda: put(keep_ref))
        pl.when(core_ref[0] != maker)(lambda: put(give_ref))


def grams(core, user_counts, item_counts, user_table, item_table):
    packed = jax.ShapeDtypeStruct((36 * NB, NB), F32)
    return pl.pallas_call(
        gram_kernel,
        out_shape=(packed, packed),
        in_specs=[SM, VM, VM, VM, VM],
        out_specs=(VM, VM),
        scratch_shapes=[pltpu.VMEM((16, NB), F32), pltpu.VMEM((N, N), F32)],
        compiler_params=PARAMS,
        cost_estimate=pl.CostEstimate(flops=1 << 33, bytes_accessed=10 << 20, transcendentals=0),
        name="grams",
    )(core, user_counts, item_counts, user_table, item_table)


def spread_rows(src, dst, base):
    def tile(r, _):
        at = pl.multiple_of(r * 16, 16)
        for c in range(KB):
            dst[pl.ds((base + at) * KB + c, 16, stride=KB), :] = src[pl.ds(at, 16), NB * c:NB * (c + 1)].astype(F32)
        return 0

    lax.fori_loop(0, src.shape[0] // 16, tile, 0)


def gather_rows(src, dst):
    def tile(r, _):
        at = pl.multiple_of(r * 16, 16)
        for c in range(KB):
            dst[pl.ds(at, 16), NB * c:NB * (c + 1)] = src[pl.ds(at * KB + c, 16, stride=KB), :].astype(BF16)
        return 0

    lax.fori_loop(0, dst.shape[0] // 16, tile, 0)


def cross_kernel(core_ref, at_ref, col_ref, i_ref, *refs, groups, add, halves):
    tables, refs = refs[:sum(groups)], refs[sum(groups):]
    if add:
        old_ref, refs = refs[0], refs[1:]
    if halves:
        keep_ref, give_ref, uf, itf, pu, pi, panel, panel_i, out_ref = refs
    else:
        out_ref, uf, itf, pu, pi, panel, panel_i = refs
    spread_rows(i_ref, itf, 0)
    users = N
    uf[users * KB:, :] = jnp.zeros((KB, NB), F32)

    def group(g, _):
        first = 0
        for j, n in enumerate(groups):
            @pl.when(g == j)
            def _(first=first, n=n):
                base = 0
                for t in tables[first:first + n]:
                    spread_rows(t, uf, base)
                    base += t.shape[0]

            first += n

        def move(b, _):
            for k in range(8):
                s = b * 8 + k
                u = at_ref[g * SLOTS + s]
                i = col_ref[g * SLOTS + s]
                to = pl.ds(pl.multiple_of(s * KB, KB), KB)
                pu[to, :] = uf[pl.ds(pl.multiple_of(u * KB, KB), KB), :]
                pi[to, :] = itf[pl.ds(pl.multiple_of(i * KB, KB), KB), :]
            return 0

        lax.fori_loop(0, SLOTS // 8, move, 0)
        gather_rows(pu, panel)
        gather_rows(pi, panel_i)

        def block(b, _):
            rows = pl.ds(pl.multiple_of(b * 256, 256), 256)
            got = tdot(panel_i[:, rows], panel[...])
            if add and len(groups) == 1:
                out_ref[rows, :] = old_ref[rows, :] + got
            else:
                @pl.when(g == 0)
                def _():
                    out_ref[rows, :] = old_ref[rows, :] + got if add else got

                @pl.when(g > 0)
                def _():
                    out_ref[rows, :] = out_ref[rows, :] + got
            return 0

        lax.fori_loop(0, N // 256, block, 0)
        return 0

    lax.fori_loop(0, len(groups), group, 0)
    if halves:
        for c in range(2):
            @pl.when(core_ref[0] == c)
            def _(c=c):
                keep_ref[...] = out_ref[c * N // 2:(c + 1) * N // 2, :]
                give_ref[...] = out_ref[(1 - c) * N // 2:(2 - c) * N // 2, :]


def cross(core, at, cols, item_table, tables, groups, old=None, halves=False):
    items = item_table.shape[0]
    more = () if old is None else (old,)
    full, half = jax.ShapeDtypeStruct((N, N), F32), jax.ShapeDtypeStruct((N // 2, N), F32)
    return pl.pallas_call(
        functools.partial(cross_kernel, groups=groups, add=old is not None, halves=halves),
        out_shape=(half, half) if halves else full,
        in_specs=[SM, SM, SM] + [VM] * (1 + len(tables) + len(more)),
        out_specs=(VM, VM) if halves else VM,
        scratch_shapes=[
            pltpu.VMEM(((N + 1) * KB, NB), F32),
            pltpu.VMEM((items * KB, NB), F32),
            pltpu.VMEM((SLOTS * KB, NB), F32),
            pltpu.VMEM((SLOTS * KB, NB), F32),
            pltpu.VMEM((SLOTS, N), BF16),
            pltpu.VMEM((SLOTS, N), BF16),
        ] + ([pltpu.VMEM((N, N), F32)] if halves else []),
        compiler_params=pltpu.CompilerParams(vmem_limit_bytes=56 << 20),
        cost_estimate=pl.CostEstimate(flops=len(groups) << 32, bytes_accessed=12 << 20, transcendentals=0),
        name="cross",
    )(core, at, cols, item_table, *tables, *more)


CHIPS = ("y", "z", "x")
CORE_FIRST = ("core", "y", "z", "x")


def swap(b):
    return lax.ppermute(b, "core", [(0, 1), (1, 0)])


def histogram(key, bins):
    hot = (key[None, :] // NB == jnp.arange(bins // NB, dtype=jnp.int32)[:, None]) & (key >= 0)[None, :]
    lane = key[:, None] % NB == jnp.arange(NB, dtype=jnp.int32)[None, :]
    return lax.dot_general(hot.astype(BF16), lane.astype(BF16), (((1,), (0,)), ((), ())), preferred_element_type=F32)


def chip_scatter(b):
    return jnp.sum(lax.all_to_all(b, CHIPS, 0, 0, tiled=True), 0)


def chip_gather(b):
    return lax.all_to_all(jnp.broadcast_to(b[None], (64,) + b.shape), CHIPS, 0, 0, tiled=True)


def ring(k):
    return [(i, (i + k) % 4) for i in range(4)]


def shift(b, axis, k):
    return lax.ppermute(b, axis, ring(k % 4))


def slot_lists(pair_user, pair_item, pair_owner, pair_count, items):
    slots = pair_owner.shape[0]
    capacity = slots // 2
    keep = jnp.arange(slots, dtype=jnp.int32) < pair_count[0]
    owner = jnp.where(keep, pair_owner, -1)
    hot = (owner[None, :] == jnp.arange(4, dtype=jnp.int32)[:, None]).reshape(4, slots // NB, NB)
    tri = (jnp.arange(NB)[:, None] <= jnp.arange(NB)[None, :]).astype(BF16)
    inside = lax.dot_general(hot.astype(BF16), tri, (((2,), (0,)), ((), ())), preferred_element_type=F32)
    totals = inside[:, :, -1]
    before = jnp.cumsum(totals, axis=1) - totals
    rank = jnp.where(hot, inside + before[:, :, None] - 1.0, 0.0)
    place = jnp.sum(rank, axis=0).reshape(slots).astype(jnp.int32)
    flat = jnp.where(keep, owner * capacity + place, -1)
    code = pair_user * items + pair_item + 1
    spots = jnp.arange(4 * capacity, dtype=jnp.int32)
    return jnp.sum(jnp.where(flat[None, :] == spots[:, None], code[None, :], 0), axis=1).reshape(4, capacity)


def body(user_table, item_table, pair_user, pair_item, pair_owner, pair_count):
    users, width = user_table.shape
    items = item_table.shape[0]
    slots = pair_user.shape[0]
    total = float(slots * 128)
    core, x = lax.axis_index("core"), lax.axis_index("x")
    flag = core.reshape(1)

    codes = slot_lists(pair_user, pair_item, pair_owner, pair_count, items)
    named = codes > 0
    want = jnp.stack([jnp.where(named, (codes - 1) // items, -1), jnp.where(named, (codes - 1) % items, 0)], 1)
    got = lax.all_to_all(want, "x", 0, 0, tiled=True)
    lists = jnp.concatenate([lax.dynamic_slice_in_dim(got, (x + k) % 4, 1, 0) for k in (0, 3, 1, 2)], 0)
    rows, cols = lists[:, 0].reshape(-1), lists[:, 1].reshape(-1)

    user_table_sent, want = lax.optimization_barrier((user_table, want))
    left, right = shift(user_table_sent, "x", 1), shift(user_table_sent, "x", -1)
    far_a, far_b = shift(left[:users // 2], "x", 1), shift(right[users // 2:], "x", -1)

    keep = jnp.arange(slots, dtype=jnp.int32) < pair_count[0]
    user_counts = histogram(jnp.where(keep, pair_user, -1), users)
    item_counts = histogram(jnp.where(rows >= 0, cols, -1), items)
    keep_half, give_half = grams(flag, user_counts, item_counts, user_table, item_table)
    mine = keep_half + swap(give_half)
    mine = chip_scatter(mine.reshape(64, 72, NB))
    packed = chip_gather(mine).reshape(36 * NB, NB)

    spot = jnp.where(rows >= 0, rows, users)
    n = codes.shape[1]
    ct = cross(flag, spot[:n], cols[:n], item_table, (user_table,), (1,))
    ct = cross(flag, spot[n:3 * n], cols[n:3 * n], item_table, (left, right), (1, 1), ct)
    half, give = cross(flag, spot[3 * n:], cols[3 * n:], item_table, (far_a, far_b), (2,), ct, halves=True)
    half = half + swap(give)
    ct = chip_scatter(half.reshape(64, 8, width))

    mine = chol(packed, 1.0 / total)
    other = swap(mine)
    r_user, left = thin(flag, ct, mine, other, 0, float(total) ** -0.5)
    left = lax.all_to_all(left, CORE_FIRST, 0, 0, tiled=True).reshape(width, NB)
    r_item, whitened = thin(flag, left, mine, other, 1)
    return (r_user, r_item, whitened)


def solution(mesh):
    fine = Mesh(mesh.devices.reshape(4, 4, 2, 4), ALL)
    placed = (P(ALL, None), P("x", None), P(ALL), P(ALL), P(ALL), P(ALL))

    return jax.shard_map(
        body,
        mesh=fine,
        in_specs=placed,
        out_specs=(P(), P(), P(ALL, None)),
        check_vma=False,
    )
```

profile of v0, /device:TPU:1, one launch (start us, length us, event | category | flops | bytes accessed | tf_op | source)
XLA Modules:
  0.0 321.8 jit_solution(12737539966914162025)
XLA Ops:
  2.6 0.8 add_select_fusion.5
  3.4 3.4 %select_reduce_fusion = s32[4096]{0:T(1024)S(1)} fusion(s32[2048]{0:T(1024)S(1)} %get-tuple-element.38, s32[2048]{0:T(1024)S(1)} %get-tuple-element.39), kind=kLoop, calls=%fused_computation | loop fusion | flops 25161728 | bytes 32768 | tf_op jit(solution)/shard_map/reduce_sum | solution.py:445
  7.6 4.8 %all-to-all-start = ((s32[4,2,1024]{2,1,0:T(2,128)}), s32[4,2,1024]{2,1,0:T(2,128)S(1)}, u32[]{:S(2)}, u32[]{:S(2)}) async-start(s32[4,2,1024]{2,1,0:T(2,128)} %copy.10), calls=%async_computation | async-start | bytes 65536 | tf_op jit(solution)/shard_map/all_to_all | solution.py:459
  13.5 3.1 all-to-all-done
  16.8 0.7 fusion.ci_ref
  17.5 2.2 copy-done.3
  19.7 11.1 %grams.1 = (f32[4608,128]{1,0:T(8,128)S(1)}, f32[4608,128]{1,0:T(8,128)S(1)}) custom-call(s32[1]{0:T(128)} %bitcast.core_ref, f32[8,128]{1,0:T(8,128)S(1)} %fusion.2.cu_ref, f32[16,128]{1,0:T(8,128)S(1)} %fusion.ci_ref, bf16[1024,1024]{1,0:T(8,128)(2,1)S(1)} %copy-done.4, bf16[2048,1024]{1,0:T(8,128)(2,1)S(1)} %copy-done.3), custom_call_target="tpu_custom_call" | custom-call | flops 8589934592 | bytes 10485760 | tf_op jit(solution)/shard_map/grams/pallas_call | solution.py:280
  30.8 2.2 collective-permute-start.5
  33.0 4.2 %collective-permute-done.5 = f32[4608,128]{1,0:T(8,128)S(1)} collective-permute-done((f32[4608,128]{1,0:T(8,128)S(1)}, f32[4608,128]{1,0:T(8,128)S(1)}, u32[]{:S(2)}, u32[]{:S(2)}) %collective-permute-start.5) | collective-permute-done | bytes 2359328 | tf_op jit(solution)/shard_map/ppermute | solution.py:405
  37.1 1.7 add.145
  38.9 9.5 %all-to-all-start.2 = ((f32[64,72,128]{2,1,0:T(8,128)}), f32[64,72,128]{2,1,0:T(8,128)}, u32[]{:S(2)}, u32[]{:S(2)}) async-start(f32[64,72,128]{2,1,0:T(8,128)} %bitcast.25), calls=%async_computation.2 | async-start | bytes 4718592 | tf_op jit(solution)/shard_map/all_to_all | solution.py:415
  48.4 2.2 collective-permute-start.2
  51.8 67.6 %collective-permute-done.2.refs_1_ = bf16[1024,1024]{1,0:T(8,128)(2,1)} collective-permute-done((bf16[1024,1024]{1,0:T(8,128)(2,1)S(1)}, bf16[1024,1024]{1,0:T(8,128)(2,1)}, u32[]{:S(2)}, u32[]{:S(2)}) %collective-permute-start.2) | collective-permute-done | bytes 2097184 | tf_op jit(solution)/shard_map/ppermute | solution.py:427
  119.5 1.3 slice.66
  120.8 1.9 collective-permute-start.3
  122.7 2.3 slice.65
  124.9 1.8 reduce_sum.39
  126.7 1.6 broadcast_in_dim.37
  128.3 9.6 %all-to-all-start.3 = ((f32[64,72,128]{2,1,0:T(8,128)}), f32[64,72,128]{2,1,0:T(8,128)S(1)}, u32[]{:S(2)}, u32[]{:S(2)}) async-start(f32[64,72,128]{2,1,0:T(8,128)} %broadcast_in_dim.37), calls=%async_computation.3 | async-start | bytes 4718592 | tf_op jit(solution)/shard_map/all_to_all | solution.py:419
  137.9 15.6 %cross.3.refs_2_ = f32[1024,1024]{1,0:T(8,128)} custom-call(s32[1]{0:T(128)} %bitcast.core_ref, s32[1024]{0:T(1024)} %get-tuple-element.34.at_ref, s32[1024]{0:T(1024)} %bitcast.33, bf16[2048,1024]{1,0:T(8,128)(2,1)} %i_ref.7, bf16[1024,1024]{1,0:T(8,128)(2,1)} %u_ref.1), custom_call_target="tpu_custom_call" | custom-call | flops 4294967296 | bytes 12582912 | tf_op jit(solution)/shard_map/cross/pallas_call | solution.py:381
  154.7 27.5 %cross.4.refs_2_ = f32[1024,1024]{1,0:T(8,128)} custom-call(s32[1]{0:T(128)} %bitcast.core_ref, s32[2048]{0:T(1024)} %slice.67.at_ref, s32[2048]{0:T(1024)} %bitcast.31, bf16[2048,1024]{1,0:T(8,128)(2,1)} %i_ref.7, bf16[1024,1024]{1,0:T(8,128)(2,1)} %collective-permute-done.refs_0_, bf16[1024,1024]{1,0:T(8,128)(2,1)} %collective-permute-done.2.refs_1_, ...), custom_call_target="tpu_custom_call" | custom-call | flops 8589934592 | bytes 12582912 | tf_op jit(solution)/shard_map/cross/pallas_call | solution.py:381
  182.2 17.1 %cross.5 = (f32[512,1024]{1,0:T(8,128)}, f32[512,1024]{1,0:T(8,128)}) custom-call(s32[1]{0:T(128)} %bitcast.core_ref, s32[1024]{0:T(1024)} %get-tuple-element.35.at_ref, s32[1024]{0:T(1024)} %bitcast.32, bf16[2048,1024]{1,0:T(8,128)(2,1)} %i_ref.7, bf16[512,1024]{1,0:T(8,128)(2,1)} %collective-permute-done.1.refs_0_, ...), custom_call_target="tpu_custom_call" | custom-call | flops 4294967296 | bytes 12582912 | tf_op jit(solution)/shard_map/cross/pallas_call | solution.py:381
  199.3 2.4 collective-permute-start.4
  201.7 1.4 copy-done.1
  203.1 1.7 copy-done.2
  204.7 35.4 %chol.1.mine_ref = f32[5632,128]{1,0:T(8,128)S(1)} custom-call(f32[4608,128]{1,0:T(8,128)S(1)} %bitcast.24), custom_call_target="tpu_custom_call" | custom-call | flops 8589934592 | bytes 8388608 | tf_op jit(solution)/shard_map/chol/pallas_call | solution.py:153
  240.2 2.9 add_bitcast_fusion
  243.2 40.3 %all_to_all.25 = f32[64,8,1024]{2,1,0:T(8,128)} all-to-all(f32[64,8,1024]{2,1,0:T(8,128)S(1)} %add_bitcast_fusion), channel_id=1, replica_groups=mesh['y'=4,'z'=4,'core'=2,'x'=4] {'y','z','x'}, dimensions={0} | all-to-all | bytes 4194304 | tf_op jit(solution)/shard_map/all_to_all | solution.py:415
  283.5 2.3 reduce_sum.38.y_ref
  285.8 8.4 %thin.2 = (f32[1024,1024]{1,0:T(8,128)}, f32[128,8,128]{2,1,0:T(8,128)}) custom-call(s32[1]{0:T(128)} %bitcast.core_ref, f32[8,1024]{1,0:T(8,128)} %reduce_sum.38.y_ref, f32[5632,128]{1,0:T(8,128)} %copy-done, f32[5632,128]{1,0:T(8,128)} %collective-permute-done.6.other_ref), custom_call_target="tpu_custom_call" | custom-call | tf_op jit(solution)/shard_map/thin/pallas_call | solution.py:227
  294.2 19.7 %all_to_all.26 = f32[128,8,128]{2,1,0:T(8,128)} all-to-all(f32[128,8,128]{2,1,0:T(8,128)} %get-tuple-element.18), channel_id=1, replica_groups=mesh['y'=4,'z'=4,'core'=2,'x'=4] {'core','y','z','x'}, dimensions={0} | all-to-all | bytes 1048576 | tf_op jit(solution)/shard_map/all_to_all | solution.py:486
  313.9 7.8 %thin.3 = (f32[1024,1024]{1,0:T(8,128)}, f32[8,1024]{1,0:T(8,128)}) custom-call(s32[1]{0:T(128)} %bitcast.core_ref, f32[1024,128]{1,0:T(8,128)} %bitcast.26, f32[5632,128]{1,0:T(8,128)} %copy-done, f32[5632,128]{1,0:T(8,128)} %collective-permute-done.6.other_ref), custom_call_target="tpu_custom_call" | custom-call | tf_op jit(solution)/shard_map/thin/pallas_call | solution.py:227
  (43 shorter events, 5.7 us)
Async XLA Ops:
  0.6 16.9 %copy-start.4 = (bf16[1024,1024]{1,0:T(8,128)(2,1)S(1)}, bf16[1024,1024]{1,0:T(8,128)(2,1)}, u32[]{:S(2)}) copy-start(bf16[1024,1024]{1,0:T(8,128)(2,1)} %u_ref.1) | copy-start | bytes 6291460
  7.6 9.1 %all-to-all-start = ((s32[4,2,1024]{2,1,0:T(2,128)}), s32[4,2,1024]{2,1,0:T(2,128)S(1)}, u32[]{:S(2)}, u32[]{:S(2)}) async-start(s32[4,2,1024]{2,1,0:T(2,128)} %copy.10), calls=%async_computation | async-start | bytes 65536 | tf_op jit(solution)/shard_map/all_to_all | solution.py:459
  17.5 2.2 copy-start.3
  30.8 6.3 %collective-permute-start.5 = (f32[4608,128]{1,0:T(8,128)S(1)}, f32[4608,128]{1,0:T(8,128)S(1)}, u32[]{:S(2)}, u32[]{:S(2)}) collective-permute-start(f32[4608,128]{1,0:T(8,128)S(1)} %get-tuple-element.16), channel_id=1, source_target_pairs={{0,4},{4,0},{1,5},{5,1},{2,6},{6,2},{3,7},{7,3},{8,12},{12,8},{9,1... | collective-permute-start | bytes 7077896 | tf_op jit(solution)/shard_map/ppermute | solution.py:405
  38.9 86.0 %all-to-all-start.2 = ((f32[64,72,128]{2,1,0:T(8,128)}), f32[64,72,128]{2,1,0:T(8,128)}, u32[]{:S(2)}, u32[]{:S(2)}) async-start(f32[64,72,128]{2,1,0:T(8,128)} %bitcast.25), calls=%async_computation.2 | async-start | bytes 4718592 | tf_op jit(solution)/shard_map/all_to_all | solution.py:415
  48.4 71.1 %collective-permute-start.2 = (bf16[1024,1024]{1,0:T(8,128)(2,1)S(1)}, bf16[1024,1024]{1,0:T(8,128)(2,1)}, u32[]{:S(2)}, u32[]{:S(2)}) collective-permute-start(bf16[1024,1024]{1,0:T(8,128)(2,1)S(1)} %copy-done.4), channel_id=1, source_target_pairs={{0,3},{1,0},{2,1},{3,2},{4,7},{5,4},{6,5},{7,6},{8,11},{9,8},{10,9... | collective-permute-start | bytes 6291464 | tf_op jit(solution)/shard_map/ppermute | solution.py:427
  50.6 72.0 %collective-permute-start = (bf16[1024,1024]{1,0:T(8,128)(2,1)S(1)}, bf16[1024,1024]{1,0:T(8,128)(2,1)}, u32[]{:S(2)}, u32[]{:S(2)}) collective-permute-start(bf16[1024,1024]{1,0:T(8,128)(2,1)S(1)} %copy-done.4), channel_id=1, source_target_pairs={{0,1},{1,2},{2,3},{3,0},{4,5},{5,6},{6,7},{7,4},{8,9},{9,10},{10,1... | collective-permute-start | bytes 6291464 | tf_op jit(solution)/shard_map/ppermute | solution.py:427
  120.8 61.4 %collective-permute-start.3 = (bf16[512,1024]{1,0:T(8,128)(2,1)S(1)}, bf16[512,1024]{1,0:T(8,128)(2,1)}, u32[]{:S(2)}, u32[]{:S(2)}) collective-permute-start(bf16[512,1024]{1,0:T(8,128)(2,1)S(1)} %slice.66), channel_id=1, source_target_pairs={{0,3},{1,0},{2,1},{3,2},{4,7},{5,4},{6,5},{7,6},{8,11},{9,8},{10,9... | collective-permute-start | bytes 3145736 | tf_op jit(solution)/shard_map/ppermute | solution.py:427
  124.9 57.3 %collective-permute-start.1 = (bf16[512,1024]{1,0:T(8,128)(2,1)}, bf16[512,1024]{1,0:T(8,128)(2,1)}, u32[]{:S(2)}, u32[]{:S(2)}) collective-permute-start(bf16[512,1024]{1,0:T(8,128)(2,1)} %slice.65), channel_id=1, source_target_pairs={{0,1},{1,2},{2,3},{3,0},{4,5},{5,6},{6,7},{7,4},{8,9},{9,10},{10,1... | collective-permute-start | bytes 3145736 | tf_op jit(solution)/shard_map/ppermute | solution.py:427
  128.3 73.3 %all-to-all-start.3 = ((f32[64,72,128]{2,1,0:T(8,128)}), f32[64,72,128]{2,1,0:T(8,128)S(1)}, u32[]{:S(2)}, u32[]{:S(2)}) async-start(f32[64,72,128]{2,1,0:T(8,128)} %broadcast_in_dim.37), calls=%async_computation.3 | async-start | bytes 4718592 | tf_op jit(solution)/shard_map/all_to_all | solution.py:419
  199.3 41.0 %collective-permute-start.4 = (f32[512,1024]{1,0:T(8,128)}, f32[512,1024]{1,0:T(8,128)}, u32[]{:S(2)}, u32[]{:S(2)}) collective-permute-start(f32[512,1024]{1,0:T(8,128)} %get-tuple-element.14), channel_id=1, source_target_pairs={{0,4},{4,0},{1,5},{5,1},{2,6},{6,2},{3,7},{7,3},{8,12},{12,8},{9,1... | collective-permute-start | bytes 6291464 | tf_op jit(solution)/shard_map/ppermute | solution.py:405
  201.7 1.4 copy-start.1
  203.1 1.7 copy-start.2
  204.7 35.5 %copy-start.5 = (f32[512,1024]{1,0:T(8,128)S(1)}, f32[512,1024]{1,0:T(8,128)}, u32[]{:S(2)}) copy-start(f32[512,1024]{1,0:T(8,128)} %get-tuple-element.13) | copy-start | bytes 6291460
  240.1 3.0 copy-start
  240.1 45.7 %collective-permute-start.6 = (f32[5632,128]{1,0:T(8,128)S(1)}, f32[5632,128]{1,0:T(8,128)}, u32[]{:S(2)}, u32[]{:S(2)}) collective-permute-start(f32[5632,128]{1,0:T(8,128)S(1)} %chol.1.mine_ref), channel_id=1, source_target_pairs={{0,4},{4,0},{1,5},{5,1},{2,6},{6,2},{3,7},{7,3},{8,12},{12,8},{9,1... | collective-permute-start | bytes 8650760 | tf_op jit(solution)/shard_map/ppermute | solution.py:405
where the time goes:
time: 323 us; the launch traced here: 322 us
  Pallas kernels  123 us (38%)
  waiting for transfers between devices  75 us (23%)
  blocking collectives  60 us (19%)
  starting transfers between devices  32.7 us (10%)
  other arithmetic  15.4 us (5%)
  local copies, waits for them, and re-layouts  13 us (4%)
    ppermute x4, waiting for transfers between devices, shift(): return lax.ppermute(b, axis, ring(k % 4))  67.7 us
    pallas_call x3, Pallas kernels, cross(): pl.pallas_call(functools.partial(cross_kernel, groups=groups, add=old is...  60.1 us
    all_to_all x1, blocking collectives, chip_scatter(): return jnp.sum(lax.all_to_all(b, CHIPS, 0, 0, tiled=True), 0)  40.3 us
    pallas_call x1, Pallas kernels, chol(): pl.pallas_call(functools.partial(chol_kernel, scale), out_shape=jax.Shape...  35.4 us
    all_to_all x1, blocking collectives, body(): left = lax.all_to_all(left, CORE_FIRST, 0, 0, tiled=True).reshape(width, NB)  19.7 us
    pallas_call x2, Pallas kernels, thin(): pl.pallas_call(functools.partial(thin_kernel, maker=maker, scale=scale),...  16.2 us
    pallas_call x1, Pallas kernels, grams(): pl.pallas_call(gram_kernel, out_shape=(packed, packed), in_specs=[SM, VM,...  11.1 us
    all_to_all x1, starting transfers between devices, chip_gather(): lax.all_to_all(jnp.broadcast_to(b[None], (64,) + b.shape), CHIPS, 0, 0, t...  9.59 us
  transfers between devices with their start and end apart: 10, of which 3 were waited for; matrix products, arithmetic and copies ran while one was open for 5% of the time, Pallas kernels for 30%

commit v1 on v0

--- a/solution.py
+++ b/solution.py
@@ -162,10 +162,18 @@
             pltpu.VMEM((8 * 8, NB), F32),
             pltpu.SemaphoreType.DMA((KB,)),
         ],
-        compiler_params=PARAMS,
+        compiler_params=pltpu.CompilerParams(vmem_limit_bytes=60 << 20),
         cost_estimate=pl.CostEstimate(flops=1 << 33, bytes_accessed=8 << 20, transcendentals=0),
         name="chol",
     )(packed)
+
+
+def small_dot(y, b, cb):
+    low = y - y.astype(BF16).astype(F32)
+    tail = low - low.astype(BF16).astype(F32)
+    rows = jnp.concatenate([y, low, tail, jnp.zeros_like(y)], 0).astype(BF16)
+    p, q, t = [lax.dot_general(rows, part, (((1,), (cb,)), ((), ())), preferred_element_type=F32) for part in parts(b)]
+    return p[:8] + ((p[8:16] + q[:8]) + (p[16:24] + q[8:16] + t[:8]))
 
 
 def place(m):
@@ -202,7 +210,7 @@
     inverses(mine_ref).wait()
     for k in range(KB):
         lo, hi = k * NB, (k + 1) * NB
-        yk = dot(y[:, lo:hi], w[lo:hi, :], 1, 1)
+        yk = small_dot(y[:, lo:hi], w[lo:hi, :], 1)
         if maker:
             out_ref[:, lo:hi] = yk
         else:
@@ -213,7 +221,7 @@
         fetch(mine_ref, k).wait()
         blocks = [rp[START[k, j]:START[k, j] + NB, :] for j in range(k, KB)]
         if hi < N:
-            y[:, hi:] = y[:, hi:] - dot(yk, jnp.concatenate(blocks[1:], 1), 1, 0)
+            y[:, hi:] = y[:, hi:] - small_dot(yk, jnp.concatenate(blocks[1:], 1), 0)
             r[hi:, lo:hi] = jnp.zeros((N - hi, NB), F32)
         for j in range(k, KB):
             r[lo:hi, NB * j:NB * (j + 1)] = blocks[j - k]
@@ -289,11 +297,11 @@
     )(core, user_counts, item_counts, user_table, item_table)
 
 
-def spread_rows(src, dst, base):
+def spread_rows(src, dst):
     def tile(r, _):
         at = pl.multiple_of(r * 16, 16)
         for c in range(KB):
-            dst[pl.ds((base + at) * KB + c, 16, stride=KB), :] = src[pl.ds(at, 16), NB * c:NB * (c + 1)].astype(F32)
+            dst[pl.ds(at * KB + c, 16, stride=KB), :] = src[pl.ds(at, 16), NB * c:NB * (c + 1)].astype(F32)
         return 0
 
     lax.fori_loop(0, src.shape[0] // 16, tile, 0)
@@ -310,28 +318,47 @@
 
 
 def cross_kernel(core_ref, at_ref, col_ref, i_ref, *refs, groups, add, halves):
-    tables, refs = refs[:sum(groups)], refs[sum(groups):]
+    count = sum(groups)
+    tables, refs = refs[:count], refs[count:]
     if add:
         old_ref, refs = refs[0], refs[1:]
-    if halves:
-        keep_ref, give_ref, uf, itf, pu, pi, panel, panel_i, out_ref = refs
-    else:
-        out_ref, uf, itf, pu, pi, panel, panel_i = refs
-    spread_rows(i_ref, itf, 0)
-    users = N
-    uf[users * KB:, :] = jnp.zeros((KB, NB), F32)
+    outs, refs = refs[:1 + halves], refs[1 + halves:]
+    ib, ub, uf, itf, pu, pi, panel, panel_i, acc, got_i, got_u, got_old, left = refs
+    last = len(groups) - 1
+    spots = [(g, t) for g, n in enumerate(groups) for t in range(n)]
+
+    def item_copy():
+        return pltpu.make_async_copy(i_ref, ib, got_i)
+
+    def old_copy():
+        return pltpu.make_async_copy(old_ref, acc, got_old)
+
+    def table_copy(n):
+        g, t = spots[n]
+        rows = tables[n].shape[0]
+        return pltpu.make_async_copy(tables[n], ub.at[g, pl.ds(t * rows, rows), :], got_u.at[n])
+
+    def leave(b, ref, to):
+        rows = pl.ds(pl.multiple_of(b * 256, 256), 256)
+        return pltpu.make_async_copy(acc.at[rows, :], ref.at[pl.ds(pl.multiple_of(to * 256, 256), 256), :], left.at[b])
+
+    item_copy().start()
+    for n in range(count):
+        table_copy(n).start()
+    if add:
+        old_copy().start()
+    item_copy().wait()
+    spread_rows(ib, itf)
+    uf[N * KB:, :] = jnp.zeros((KB, NB), F32)
 
     def group(g, _):
-        first = 0
-        for j, n in enumerate(groups):
+        for j in range(len(groups)):
             @pl.when(g == j)
-            def _(first=first, n=n):
-                base = 0
-                for t in tables[first:first + n]:
-                    spread_rows(t, uf, base)
-                    base += t.shape[0]
-
-            first += n
+            def _(j=j):
+                for n in range(count):
+                    if spots[n][0] == j:
+                        table_copy(n).wait()
+                spread_rows(ub.at[j], uf)
 
         def move(b, _):
             for k in range(8):
@@ -346,52 +373,64 @@
         lax.fori_loop(0, SLOTS // 8, move, 0)
         gather_rows(pu, panel)
         gather_rows(pi, panel_i)
+        if add:
+            @pl.when(g == 0)
+            def _():
+                old_copy().wait()
 
         def block(b, _):
             rows = pl.ds(pl.multiple_of(b * 256, 256), 256)
             got = tdot(panel_i[:, rows], panel[...])
-            if add and len(groups) == 1:
-                out_ref[rows, :] = old_ref[rows, :] + got
+            if add:
+                acc[rows, :] = acc[rows, :] + got
             else:
-                @pl.when(g == 0)
-                def _():
-                    out_ref[rows, :] = old_ref[rows, :] + got if add else got
-
-                @pl.when(g > 0)
-                def _():
-                    out_ref[rows, :] = out_ref[rows, :] + got
+                acc[rows, :] = got
+
+            @pl.when(g == last)
+            def _():
+                if halves:
+                    mine = b // 2 == core_ref[0]
+                    pl.when(mine)(lambda: leave(b, outs[0], b % 2).start())
+                    pl.when(jnp.logical_not(mine))(lambda: leave(b, outs[1], b % 2).start())
+                else:
+                    leave(b, outs[0], b).start()
+
             return 0
 
         lax.fori_loop(0, N // 256, block, 0)
         return 0
 
     lax.fori_loop(0, len(groups), group, 0)
-    if halves:
-        for c in range(2):
-            @pl.when(core_ref[0] == c)
-            def _(c=c):
-                keep_ref[...] = out_ref[c * N // 2:(c + 1) * N // 2, :]
-                give_ref[...] = out_ref[(1 - c) * N // 2:(2 - c) * N // 2, :]
+    for b in range(N // 256):
+        leave(b, outs[0], 0).wait()
 
 
 def cross(core, at, cols, item_table, tables, groups, old=None, halves=False):
+    assert old is not None or len(groups) == 1
     items = item_table.shape[0]
     more = () if old is None else (old,)
     full, half = jax.ShapeDtypeStruct((N, N), F32), jax.ShapeDtypeStruct((N // 2, N), F32)
     return pl.pallas_call(
         functools.partial(cross_kernel, groups=groups, add=old is not None, halves=halves),
         out_shape=(half, half) if halves else full,
-        in_specs=[SM, SM, SM] + [VM] * (1 + len(tables) + len(more)),
-        out_specs=(VM, VM) if halves else VM,
+        in_specs=[SM, SM, SM] + [HBM] * (1 + len(tables) + len(more)),
+        out_specs=(HBM, HBM) if halves else HBM,
         scratch_shapes=[
+            pltpu.VMEM((items, N), BF16),
+            pltpu.VMEM((len(groups), N, N), BF16),
             pltpu.VMEM(((N + 1) * KB, NB), F32),
             pltpu.VMEM((items * KB, NB), F32),
             pltpu.VMEM((SLOTS * KB, NB), F32),
             pltpu.VMEM((SLOTS * KB, NB), F32),
             pltpu.VMEM((SLOTS, N), BF16),
             pltpu.VMEM((SLOTS, N), BF16),
-        ] + ([pltpu.VMEM((N, N), F32)] if halves else []),
-        compiler_params=pltpu.CompilerParams(vmem_limit_bytes=56 << 20),
+            pltpu.VMEM((N, N), F32),
+            pltpu.SemaphoreType.DMA,
+            pltpu.SemaphoreType.DMA((len(tables),)),
+            pltpu.SemaphoreType.DMA,
+            pltpu.SemaphoreType.DMA((N // 256,)),
+        ],
+        compiler_params=pltpu.CompilerParams(vmem_limit_bytes=60 << 20),
         cost_estimate=pl.CostEstimate(flops=len(groups) << 32, bytes_accessed=12 << 20, transcendentals=0),
         name="cross",
     )(core, at, cols, item_table, *tables, *more)

time: 323 us -> 313 us (0.969)
  Pallas kernels: 123 us -> 116 us
    pallas_call x3, Pallas kernels: 60.1 us -> 54.3 us  [cross(): pl.pallas_call(functools.partial(cross_kernel, groups=groups, add=old is...]
  transfers between devices with their start and end apart: 10 -> 10, of which waited for: 3 -> 3; matrix products, arithmetic and copies ran while one was open for 5% -> 5% of each run, Pallas kernels for 30% -> 29%
where the time goes in v1:
time: 313 us; the launch traced here: 312 us
  Pallas kernels  116 us (37%)
  waiting for transfers between devices  75 us (24%)
  blocking collectives  59.4 us (19%)
  starting transfers between devices  33 us (11%)
  other arithmetic  15.2 us (5%)
  local copies, waits for them, and re-layouts  10.2 us (3%)
    ppermute x4, waiting for transfers between devices, shift(): return lax.ppermute(b, axis, ring(k % 4))  67.7 us
    pallas_call x3, Pallas kernels, cross(): pl.pallas_call(functools.partial(cross_kernel, groups=groups, add=old is...  54.3 us
    all_to_all x1, blocking collectives, chip_scatter(): return jnp.sum(lax.all_to_all(b, CHIPS, 0, 0, tiled=True), 0)  38.6 us
    pallas_call x1, Pallas kernels, chol(): pl.pallas_call(functools.partial(chol_kernel, scale), out_shape=jax.Shape...  37.2 us
    all_to_all x1, blocking collectives, body(): left = lax.all_to_all(left, CORE_FIRST, 0, 0, tiled=True).reshape(width, NB)  20.8 us
    pallas_call x2, Pallas kernels, thin(): pl.pallas_call(functools.partial(thin_kernel, maker=maker, scale=scale),...  13.5 us
    pallas_call x1, Pallas kernels, grams(): pl.pallas_call(gram_kernel, out_shape=(packed, packed), in_specs=[SM, VM,...  11.1 us
    all_to_all x1, starting transfers between devices, chip_gather(): lax.all_to_all(jnp.broadcast_to(b[None], (64,) + b.shape), CHIPS, 0, 0, t...  9.8 us
  transfers between devices with their start and end apart: 10, of which 3 were waited for; matrix products, arithmetic and copies ran while one was open for 5% of the time, Pallas kernels for 29%

profile of v1, /device:TPU:1, one launch (start us, length us, event | category | flops | bytes accessed | tf_op | source)
XLA Modules:
  0.0 312.0 jit_solution(15575980691110873854)
XLA Ops:
  2.6 0.8 add_select_fusion.5
  3.4 3.4 %select_reduce_fusion = s32[4096]{0:T(1024)S(1)} fusion(s32[2048]{0:T(1024)S(1)} %get-tuple-element.38, s32[2048]{0:T(1024)S(1)} %get-tuple-element.39), kind=kLoop, calls=%fused_computation | loop fusion | flops 25161728 | bytes 32768 | tf_op jit(solution)/shard_map/reduce_sum | solution.py:484
  7.6 4.8 %all-to-all-start = ((s32[4,2,1024]{2,1,0:T(2,128)}), s32[4,2,1024]{2,1,0:T(2,128)S(1)}, u32[]{:S(2)}, u32[]{:S(2)}) async-start(s32[4,2,1024]{2,1,0:T(2,128)} %copy.10), calls=%async_computation | async-start | bytes 65536 | tf_op jit(solution)/shard_map/all_to_all | solution.py:498
  12.4 0.7 fusion.26
  13.5 3.1 %all-to-all-done = s32[4,2,1024]{2,1,0:T(2,128)S(1)} async-done(((s32[4,2,1024]{2,1,0:T(2,128)}), s32[4,2,1024]{2,1,0:T(2,128)S(1)}, u32[]{:S(2)}, u32[]{:S(2)}) %all-to-all-start) | async-done | bytes 32800 | tf_op jit(solution)/shard_map/all_to_all | solution.py:498
  16.8 0.7 fusion.ci_ref
  17.5 2.2 copy-done
  19.7 11.1 %grams.1 = (f32[4608,128]{1,0:T(8,128)S(1)}, f32[4608,128]{1,0:T(8,128)S(1)}) custom-call(s32[1]{0:T(128)} %bitcast.core_ref, f32[8,128]{1,0:T(8,128)S(1)} %fusion.2.cu_ref, f32[16,128]{1,0:T(8,128)S(1)} %fusion.ci_ref, bf16[1024,1024]{1,0:T(8,128)(2,1)S(1)} %copy-done.1, bf16[2048,1024]{1,0:T(8,128)(2,1)S(1)} %copy-done), custom_call_target="tpu_custom_call" | custom-call | flops 8589934592 | bytes 10485760 | tf_op jit(solution)/shard_map/grams/pallas_call | solution.py:288
  30.8 2.2 collective-permute-start.5
  33.0 4.2 %collective-permute-done.5 = f32[4608,128]{1,0:T(8,128)S(1)} collective-permute-done((f32[4608,128]{1,0:T(8,128)S(1)}, f32[4608,128]{1,0:T(8,128)S(1)}, u32[]{:S(2)}, u32[]{:S(2)}) %collective-permute-start.5) | collective-permute-done | bytes 2359328 | tf_op jit(solution)/shard_map/ppermute | solution.py:444
  37.1 1.7 add.145
  38.9 9.5 %all-to-all-start.2 = ((f32[64,72,128]{2,1,0:T(8,128)}), f32[64,72,128]{2,1,0:T(8,128)}, u32[]{:S(2)}, u32[]{:S(2)}) async-start(f32[64,72,128]{2,1,0:T(8,128)} %bitcast.24), calls=%async_computation.2 | async-start | bytes 4718592 | tf_op jit(solution)/shard_map/all_to_all | solution.py:454
  48.4 2.2 collective-permute-start.2
  51.8 67.6 %collective-permute-done.2.refs_1_ = bf16[1024,1024]{1,0:T(8,128)(2,1)} collective-permute-done((bf16[1024,1024]{1,0:T(8,128)(2,1)S(1)}, bf16[1024,1024]{1,0:T(8,128)(2,1)}, u32[]{:S(2)}, u32[]{:S(2)}) %collective-permute-start.2) | collective-permute-done | bytes 2097184 | tf_op jit(solution)/shard_map/ppermute | solution.py:466
  119.5 1.3 slice.66
  120.8 1.9 collective-permute-start.3
  122.7 1.3 slice.65
  124.1 1.8 reduce_sum.39
  125.9 1.6 broadcast_in_dim.37
  127.4 9.8 %all-to-all-start.3 = ((f32[64,72,128]{2,1,0:T(8,128)}), f32[64,72,128]{2,1,0:T(8,128)}, u32[]{:S(2)}, u32[]{:S(2)}) async-start(f32[64,72,128]{2,1,0:T(8,128)} %broadcast_in_dim.37), calls=%async_computation.3 | async-start | bytes 4718592 | tf_op jit(solution)/shard_map/all_to_all | solution.py:458
  137.3 14.6 %cross.3.refs_2_ = f32[1024,1024]{1,0:T(8,128)} custom-call(s32[1]{0:T(128)} %bitcast.core_ref, s32[1024]{0:T(1024)} %get-tuple-element.34.at_ref, s32[1024]{0:T(1024)} %bitcast.32, bf16[2048,1024]{1,0:T(8,128)(2,1)} %i_ref.7, bf16[1024,1024]{1,0:T(8,128)(2,1)} %u_ref.1), custom_call_target="tpu_custom_call" | custom-call | flops 4294967296 | bytes 12582912 | tf_op jit(solution)/shard_map/cross/pallas_call | solution.py:413
  153.1 24.7 %cross.4.refs_2_ = f32[1024,1024]{1,0:T(8,128)} custom-call(s32[1]{0:T(128)} %bitcast.core_ref, s32[2048]{0:T(1024)} %slice.67.at_ref, s32[2048]{0:T(1024)} %bitcast.30, bf16[2048,1024]{1,0:T(8,128)(2,1)} %i_ref.7, bf16[1024,1024]{1,0:T(8,128)(2,1)} %collective-permute-done.refs_0_, bf16[1024,1024]{1,0:T(8,128)(2,1)} %collective-permute-done.2.refs_1_, ...), custom_call_target="tpu_custom_call" | custom-call | flops 8589934592 | bytes 12582912 | tf_op jit(solution)/shard_map/cross/pallas_call | solution.py:413
  177.8 15.0 %cross.5 = (f32[512,1024]{1,0:T(8,128)}, f32[512,1024]{1,0:T(8,128)}) custom-call(s32[1]{0:T(128)} %bitcast.core_ref, s32[1024]{0:T(1024)} %get-tuple-element.35.at_ref, s32[1024]{0:T(1024)} %bitcast.31, bf16[2048,1024]{1,0:T(8,128)(2,1)} %i_ref.7, bf16[512,1024]{1,0:T(8,128)(2,1)} %collective-permute-done.1.refs_0_, ...), custom_call_target="tpu_custom_call" | custom-call | flops 4294967296 | bytes 12582912 | tf_op jit(solution)/shard_map/cross/pallas_call | solution.py:413
  192.8 2.4 collective-permute-start.4
  195.2 37.2 %chol.1.mine_ref = f32[5632,128]{1,0:T(8,128)} custom-call(f32[4608,128]{1,0:T(8,128)} %bitcast.12.g_ref), custom_call_target="tpu_custom_call" | custom-call | flops 8589934592 | bytes 8388608 | tf_op jit(solution)/shard_map/chol/pallas_call | solution.py:153
  232.5 1.3 copy-done.2
  233.8 2.8 add_bitcast_fusion
  236.6 38.6 %all_to_all.25 = f32[64,8,1024]{2,1,0:T(8,128)} all-to-all(f32[64,8,1024]{2,1,0:T(8,128)S(1)} %add_bitcast_fusion), channel_id=1, replica_groups=mesh['y'=4,'z'=4,'core'=2,'x'=4] {'y','z','x'}, dimensions={0} | all-to-all | bytes 4194304 | tf_op jit(solution)/shard_map/all_to_all | solution.py:454
  275.2 2.3 reduce_sum.38.y_ref
  277.6 7.0 %thin.2 = (f32[1024,1024]{1,0:T(8,128)}, f32[128,8,128]{2,1,0:T(8,128)}) custom-call(s32[1]{0:T(128)} %bitcast.core_ref, f32[8,1024]{1,0:T(8,128)} %reduce_sum.38.y_ref, f32[5632,128]{1,0:T(8,128)} %chol.1.mine_ref, f32[5632,128]{1,0:T(8,128)} %collective-permute-done.6.other_ref), custom_call_target="tpu_custom_call" | custom-call | tf_op jit(solution)/shard_map/thin/pallas_call | solution.py:235
  284.6 20.8 %all_to_all.26 = f32[128,8,128]{2,1,0:T(8,128)} all-to-all(f32[128,8,128]{2,1,0:T(8,128)} %get-tuple-element.18), channel_id=1, replica_groups=mesh['y'=4,'z'=4,'core'=2,'x'=4] {'core','y','z','x'}, dimensions={0} | all-to-all | bytes 1048576 | tf_op jit(solution)/shard_map/all_to_all | solution.py:525
  305.4 6.4 %thin.3 = (f32[1024,1024]{1,0:T(8,128)}, f32[8,1024]{1,0:T(8,128)}) custom-call(s32[1]{0:T(128)} %bitcast.core_ref, f32[1024,128]{1,0:T(8,128)} %bitcast.25, f32[5632,128]{1,0:T(8,128)} %chol.1.mine_ref, f32[5632,128]{1,0:T(8,128)} %collective-permute-done.6.other_ref), custom_call_target="tpu_custom_call" | custom-call | tf_op jit(solution)/shard_map/thin/pallas_call | solution.py:235
  (37 shorter events, 5.0 us)
Async XLA Ops:
  0.6 16.9 %copy-start.1 = (bf16[1024,1024]{1,0:T(8,128)(2,1)S(1)}, bf16[1024,1024]{1,0:T(8,128)(2,1)}, u32[]{:S(2)}) copy-start(bf16[1024,1024]{1,0:T(8,128)(2,1)} %u_ref.1) | copy-start | bytes 6291460
  7.6 9.1 %all-to-all-start = ((s32[4,2,1024]{2,1,0:T(2,128)}), s32[4,2,1024]{2,1,0:T(2,128)S(1)}, u32[]{:S(2)}, u32[]{:S(2)}) async-start(s32[4,2,1024]{2,1,0:T(2,128)} %copy.10), calls=%async_computation | async-start | bytes 65536 | tf_op jit(solution)/shard_map/all_to_all | solution.py:498
  17.5 2.2 copy-start
  30.8 6.3 %collective-permute-start.5 = (f32[4608,128]{1,0:T(8,128)S(1)}, f32[4608,128]{1,0:T(8,128)S(1)}, u32[]{:S(2)}, u32[]{:S(2)}) collective-permute-start(f32[4608,128]{1,0:T(8,128)S(1)} %get-tuple-element.16), channel_id=1, source_target_pairs={{0,4},{4,0},{1,5},{5,1},{2,6},{6,2},{3,7},{7,3},{8,12},{12,8},{9,1... | collective-permute-start | bytes 7077896 | tf_op jit(solution)/shard_map/ppermute | solution.py:444
  38.9 85.2 %all-to-all-start.2 = ((f32[64,72,128]{2,1,0:T(8,128)}), f32[64,72,128]{2,1,0:T(8,128)}, u32[]{:S(2)}, u32[]{:S(2)}) async-start(f32[64,72,128]{2,1,0:T(8,128)} %bitcast.24), calls=%async_computation.2 | async-start | bytes 4718592 | tf_op jit(solution)/shard_map/all_to_all | solution.py:454
  48.4 71.1 %collective-permute-start.2 = (bf16[1024,1024]{1,0:T(8,128)(2,1)S(1)}, bf16[1024,1024]{1,0:T(8,128)(2,1)}, u32[]{:S(2)}, u32[]{:S(2)}) collective-permute-start(bf16[1024,1024]{1,0:T(8,128)(2,1)S(1)} %copy-done.1), channel_id=1, source_target_pairs={{0,3},{1,0},{2,1},{3,2},{4,7},{5,4},{6,5},{7,6},{8,11},{9,8},{10,9... | collective-permute-start | bytes 6291464 | tf_op jit(solution)/shard_map/ppermute | solution.py:466
  50.6 72.0 %collective-permute-start = (bf16[1024,1024]{1,0:T(8,128)(2,1)S(1)}, bf16[1024,1024]{1,0:T(8,128)(2,1)}, u32[]{:S(2)}, u32[]{:S(2)}) collective-permute-start(bf16[1024,1024]{1,0:T(8,128)(2,1)S(1)} %copy-done.1), channel_id=1, source_target_pairs={{0,1},{1,2},{2,3},{3,0},{4,5},{5,6},{6,7},{7,4},{8,9},{9,10},{10,1... | collective-permute-start | bytes 6291464 | tf_op jit(solution)/shard_map/ppermute | solution.py:466
  120.8 57.0 %collective-permute-start.3 = (bf16[512,1024]{1,0:T(8,128)(2,1)S(1)}, bf16[512,1024]{1,0:T(8,128)(2,1)}, u32[]{:S(2)}, u32[]{:S(2)}) collective-permute-start(bf16[512,1024]{1,0:T(8,128)(2,1)S(1)} %slice.66), channel_id=1, source_target_pairs={{0,3},{1,0},{2,1},{3,2},{4,7},{5,4},{6,5},{7,6},{8,11},{9,8},{10,9... | collective-permute-start | bytes 3145736 | tf_op jit(solution)/shard_map/ppermute | solution.py:466
  124.0 53.8 %collective-permute-start.1 = (bf16[512,1024]{1,0:T(8,128)(2,1)S(1)}, bf16[512,1024]{1,0:T(8,128)(2,1)}, u32[]{:S(2)}, u32[]{:S(2)}) collective-permute-start(bf16[512,1024]{1,0:T(8,128)(2,1)S(1)} %slice.65), channel_id=1, source_target_pairs={{0,1},{1,2},{2,3},{3,0},{4,5},{5,6},{6,7},{7,4},{8,9},{9,10},{10,1... | collective-permute-start | bytes 3145736 | tf_op jit(solution)/shard_map/ppermute | solution.py:466
  127.4 67.8 %all-to-all-start.3 = ((f32[64,72,128]{2,1,0:T(8,128)}), f32[64,72,128]{2,1,0:T(8,128)}, u32[]{:S(2)}, u32[]{:S(2)}) async-start(f32[64,72,128]{2,1,0:T(8,128)} %broadcast_in_dim.37), calls=%async_computation.3 | async-start | bytes 4718592 | tf_op jit(solution)/shard_map/all_to_all | solution.py:458
  192.8 39.7 %collective-permute-start.4 = (f32[512,1024]{1,0:T(8,128)}, f32[512,1024]{1,0:T(8,128)S(1)}, u32[]{:S(2)}, u32[]{:S(2)}) collective-permute-start(f32[512,1024]{1,0:T(8,128)} %get-tuple-element.14), channel_id=1, source_target_pairs={{0,4},{4,0},{1,5},{5,1},{2,6},{6,2},{3,7},{7,3},{8,12},{12,8},{9,1... | collective-permute-start | bytes 6291464 | tf_op jit(solution)/shard_map/ppermute | solution.py:444
  232.4 45.2 %collective-permute-start.6 = (f32[5632,128]{1,0:T(8,128)}, f32[5632,128]{1,0:T(8,128)}, u32[]{:S(2)}, u32[]{:S(2)}) collective-permute-start(f32[5632,128]{1,0:T(8,128)} %chol.1.mine_ref), channel_id=1, source_target_pairs={{0,4},{4,0},{1,5},{5,1},{2,6},{6,2},{3,7},{7,3},{8,12},{12,8},{9,1... | collective-permute-start | bytes 8650760 | tf_op jit(solution)/shard_map/ppermute | solution.py:444
  232.5 1.3 copy-start.2

commit v2 on v1

--- a/solution.py
+++ b/solution.py
@@ -317,7 +317,7 @@
     lax.fori_loop(0, dst.shape[0] // 16, tile, 0)
 
 
-def cross_kernel(core_ref, at_ref, col_ref, i_ref, *refs, groups, add, halves):
+def cross_kernel(core_ref, at_ref, col_ref, i_ref, *refs, groups, first, add, halves):
     count = sum(groups)
     tables, refs = refs[:count], refs[count:]
     if add:
@@ -360,11 +360,13 @@
                         table_copy(n).wait()
                 spread_rows(ub.at[j], uf)
 
+        base = core_ref[1 + first + g] * SLOTS
+
         def move(b, _):
             for k in range(8):
                 s = b * 8 + k
-                u = at_ref[g * SLOTS + s]
-                i = col_ref[g * SLOTS + s]
+                u = at_ref[base + s]
+                i = col_ref[base + s]
                 to = pl.ds(pl.multiple_of(s * KB, KB), KB)
                 pu[to, :] = uf[pl.ds(pl.multiple_of(u * KB, KB), KB), :]
                 pi[to, :] = itf[pl.ds(pl.multiple_of(i * KB, KB), KB), :]
@@ -405,13 +407,13 @@
         leave(b, outs[0], 0).wait()
 
 
-def cross(core, at, cols, item_table, tables, groups, old=None, halves=False):
+def cross(flag, at, cols, item_table, tables, groups, first, old=None, halves=False):
     assert old is not None or len(groups) == 1
     items = item_table.shape[0]
     more = () if old is None else (old,)
     full, half = jax.ShapeDtypeStruct((N, N), F32), jax.ShapeDtypeStruct((N // 2, N), F32)
     return pl.pallas_call(
-        functools.partial(cross_kernel, groups=groups, add=old is not None, halves=halves),
+        functools.partial(cross_kernel, groups=groups, first=first, add=old is not None, halves=halves),
         out_shape=(half, half) if halves else full,
         in_specs=[SM, SM, SM] + [HBM] * (1 + len(tables) + len(more)),
         out_specs=(HBM, HBM) if halves else HBM,
@@ -433,7 +435,7 @@
         compiler_params=pltpu.CompilerParams(vmem_limit_bytes=60 << 20),
         cost_estimate=pl.CostEstimate(flops=len(groups) << 32, bytes_accessed=12 << 20, transcendentals=0),
         name="cross",
-    )(core, at, cols, item_table, *tables, *more)
+    )(flag, at, cols, item_table, *tables, *more)
 
 
 CHIPS = ("y", "z", "x")
@@ -490,14 +492,13 @@
     slots = pair_user.shape[0]
     total = float(slots * 128)
     core, x = lax.axis_index("core"), lax.axis_index("x")
-    flag = core.reshape(1)
+    flag = jnp.stack([core] + [(x + k) % 4 for k in (0, 3, 1, 2)])
 
     codes = slot_lists(pair_user, pair_item, pair_owner, pair_count, items)
     named = codes > 0
     want = jnp.stack([jnp.where(named, (codes - 1) // items, -1), jnp.where(named, (codes - 1) % items, 0)], 1)
     got = lax.all_to_all(want, "x", 0, 0, tiled=True)
-    lists = jnp.concatenate([lax.dynamic_slice_in_dim(got, (x + k) % 4, 1, 0) for k in (0, 3, 1, 2)], 0)
-    rows, cols = lists[:, 0].reshape(-1), lists[:, 1].reshape(-1)
+    rows, cols = got[:, 0].reshape(-1), got[:, 1].reshape(-1)
 
     user_table_sent, want = lax.optimization_barrier((user_table, want))
     left, right = shift(user_table_sent, "x", 1), shift(user_table_sent, "x", -1)
@@ -512,10 +513,9 @@
     packed = chip_gather(mine).reshape(36 * NB, NB)
 
     spot = jnp.where(rows >= 0, rows, users)
-    n = codes.shape[1]
-    ct = cross(flag, spot[:n], cols[:n], item_table, (user_table,), (1,))
-    ct = cross(flag, spot[n:3 * n], cols[n:3 * n], item_table, (left, right), (1, 1), ct)
-    half, give = cross(flag, spot[3 * n:], cols[3 * n:], item_table, (far_a, far_b), (2,), ct, halves=True)
+    ct = cross(flag, spot, cols, item_table, (user_table,), (1,), 0)
+    ct = cross(flag, spot, cols, item_table, (left, right), (1, 1), 1, ct)
+    half, give = cross(flag, spot, cols, item_table, (far_a, far_b), (2,), 3, ct, halves=True)
     half = half + swap(give)
     ct = chip_scatter(half.reshape(64, 8, width))
 

time: 313 us -> 317 us (1.013)
    unnamed x6 -> x18, local copies, waits for them, and re-layouts: 3.51 us -> 7.36 us
  transfers between devices with their start and end apart: 10 -> 10, of which waited for: 3 -> 3; matrix products, arithmetic and copies ran while one was open for 5% -> 3% of each run, Pallas kernels for 29% -> 30%
where the time goes in v2:
time: 317 us; the launch traced here: 316 us
  Pallas kernels  119 us (38%)
  waiting for transfers between devices  76 us (24%)
  blocking collectives  59.5 us (19%)
  starting transfers between devices  32.9 us (10%)
  other arithmetic  15 us (5%)
  local copies, waits for them, and re-layouts  11 us (3%)
    ppermute x4, waiting for transfers between devices, shift(): return lax.ppermute(b, axis, ring(k % 4))  68.7 us
    pallas_call x3, Pallas kernels, cross(): pl.pallas_call(functools.partial(cross_kernel, groups=groups, first=first...  56.3 us
    all_to_all x1, blocking collectives, chip_scatter(): return jnp.sum(lax.all_to_all(b, CHIPS, 0, 0, tiled=True), 0)  38.7 us
    pallas_call x1, Pallas kernels, chol(): pl.pallas_call(functools.partial(chol_kernel, scale), out_shape=jax.Shape...  37.2 us
    all_to_all x1, blocking collectives, body(): left = lax.all_to_all(left, CORE_FIRST, 0, 0, tiled=True).reshape(width, NB)  20.7 us
    pallas_call x2, Pallas kernels, thin(): pl.pallas_call(functools.partial(thin_kernel, maker=maker, scale=scale),...  13.5 us
    pallas_call x1, Pallas kernels, grams(): pl.pallas_call(gram_kernel, out_shape=(packed, packed), in_specs=[SM, VM,...  11.7 us
    all_to_all x1, starting transfers between devices, chip_scatter(): return jnp.sum(lax.all_to_all(b, CHIPS, 0, 0, tiled=True), 0)  9.64 us
  transfers between devices with their start and end apart: 10, of which 3 were waited for; matrix products, arithmetic and copies ran while one was open for 3% of the time, Pallas kernels for 30%

profile of v2, /device:TPU:1, one launch (start us, length us, event | category | flops | bytes accessed | tf_op | source)
XLA Modules:
  0.0 316.0 jit_solution(3193623583798841009)
XLA Ops:
  2.5 0.8 add_select_fusion.5
  3.2 3.4 %select_reduce_fusion = s32[4096]{0:T(1024)S(1)} fusion(s32[2048]{0:T(1024)S(1)} %get-tuple-element.30, s32[2048]{0:T(1024)S(1)} %get-tuple-element.31), kind=kLoop, calls=%fused_computation | loop fusion | flops 25161728 | bytes 32768 | tf_op jit(solution)/shard_map/reduce_sum | solution.py:486
  7.4 4.8 %all-to-all-start = ((s32[4,2,1024]{2,1,0:T(2,128)}), s32[4,2,1024]{2,1,0:T(2,128)S(1)}, u32[]{:S(2)}, u32[]{:S(2)}) async-start(s32[4,2,1024]{2,1,0:T(2,128)} %copy.10), calls=%async_computation | async-start | bytes 65536 | tf_op jit(solution)/shard_map/all_to_all | solution.py:500
  13.5 3.1 all-to-all-done
  17.2 0.7 fusion.ci_ref
  17.9 2.2 copy-done.1
  20.1 1.6 copy-done.2
  21.7 11.7 %grams.1 = (f32[4608,128]{1,0:T(8,128)S(1)}, f32[4608,128]{1,0:T(8,128)S(1)}) custom-call(s32[5]{0:T(128)S(1)} %stack.28.core_ref, f32[8,128]{1,0:T(8,128)S(1)} %fusion.2.cu_ref, f32[16,128]{1,0:T(8,128)S(1)} %fusion.ci_ref, bf16[1024,1024]{1,0:T(8,128)(2,1)S(1)} %copy-done.2, bf16[2048,1024]{1,0:T(8,128)(2,1)S(1)} %copy-done.1), custom_call_target="tpu_custom_call" | custom-call | flops 8589934592 | bytes 10485760 | tf_op jit(solution)/shard_map/grams/pallas_call | solution.py:288
  33.4 2.2 collective-permute-start.5
  35.6 4.2 %collective-permute-done.5 = f32[4608,128]{1,0:T(8,128)S(1)} collective-permute-done((f32[4608,128]{1,0:T(8,128)S(1)}, f32[4608,128]{1,0:T(8,128)S(1)}, u32[]{:S(2)}, u32[]{:S(2)}) %collective-permute-start.5) | collective-permute-done | bytes 2359328 | tf_op jit(solution)/shard_map/ppermute | solution.py:446
  39.8 1.7 add.129
  41.5 9.6 %all-to-all-start.2 = ((f32[64,72,128]{2,1,0:T(8,128)}), f32[64,72,128]{2,1,0:T(8,128)}, u32[]{:S(2)}, u32[]{:S(2)}) async-start(f32[64,72,128]{2,1,0:T(8,128)} %bitcast.25), calls=%async_computation.2 | async-start | bytes 4718592 | tf_op jit(solution)/shard_map/all_to_all | solution.py:456
  51.2 2.2 collective-permute-start.2
  53.4 68.7 %collective-permute-done.2.refs_1_ = bf16[1024,1024]{1,0:T(8,128)(2,1)S(1)} collective-permute-done((bf16[1024,1024]{1,0:T(8,128)(2,1)S(1)}, bf16[1024,1024]{1,0:T(8,128)(2,1)S(1)}, u32[]{:S(2)}, u32[]{:S(2)}) %collective-permute-start.2) | collective-permute-done | bytes 2097184 | tf_op jit(solution)/shard_map/ppermute | solution.py:468
  122.2 1.9 collective-permute-start.3
  124.1 1.1 slice.23
  126.3 1.8 reduce_sum.39
  128.2 1.6 broadcast_in_dim.37
  129.7 9.1 %all-to-all-start.3 = ((f32[64,72,128]{2,1,0:T(8,128)}), f32[64,72,128]{2,1,0:T(8,128)S(1)}, u32[]{:S(2)}, u32[]{:S(2)}) async-start(f32[64,72,128]{2,1,0:T(8,128)} %broadcast_in_dim.37), calls=%async_computation.3 | async-start | bytes 4718592 | tf_op jit(solution)/shard_map/all_to_all | solution.py:460
  138.8 15.4 %cross.3.refs_2_ = f32[1024,1024]{1,0:T(8,128)} custom-call(s32[5]{0:T(128)} %copy-done, s32[4096]{0:T(1024)} %get-tuple-element.27.at_ref, s32[4096]{0:T(1024)} %bitcast.30, bf16[2048,1024]{1,0:T(8,128)(2,1)} %i_ref.7, bf16[1024,1024]{1,0:T(8,128)(2,1)} %u_ref.1), custom_call_target="tpu_custom_call" | custom-call | flops 4294967296 | bytes 12582912 | tf_op jit(solution)/shard_map/cross/pallas_call | solution.py:415
  154.2 25.1 %cross.4.refs_2_ = f32[1024,1024]{1,0:T(8,128)} custom-call(s32[5]{0:T(128)} %copy-done, s32[4096]{0:T(1024)} %get-tuple-element.27.at_ref, s32[4096]{0:T(1024)} %bitcast.31, bf16[2048,1024]{1,0:T(8,128)(2,1)} %i_ref.7, bf16[1024,1024]{1,0:T(8,128)(2,1)} %copy-done.7, bf16[1024,1024]{1,0:T(8,128)(2,1)} %copy-done.6, f32[1024,1024]{1,0:T(8,128)} %cross.3.refs_2_), custom_call_target="tpu_custom_call" | custom-call | flops 8589934592 | bytes 12582912 | tf_op jit(solution)/shard_map/cross/pallas_call | solution.py:415
  179.3 15.8 %cross.5 = (f32[512,1024]{1,0:T(8,128)}, f32[512,1024]{1,0:T(8,128)}) custom-call(s32[5]{0:T(128)} %copy-done, s32[4096]{0:T(1024)} %get-tuple-element.27.at_ref, s32[4096]{0:T(1024)} %bitcast.32, bf16[2048,1024]{1,0:T(8,128)(2,1)} %i_ref.7, bf16[512,1024]{1,0:T(8,128)(2,1)} %collective-permute-done.1.refs_0_, ...), custom_call_target="tpu_custom_call" | custom-call | flops 4294967296 | bytes 12582912 | tf_op jit(solution)/shard_map/cross/pallas_call | solution.py:415
  195.1 2.5 collective-permute-start.4
  197.6 1.4 copy-done.5
  199.0 37.2 %chol.1.mine_ref = f32[5632,128]{1,0:T(8,128)} custom-call(f32[4608,128]{1,0:T(8,128)} %bitcast.26), custom_call_target="tpu_custom_call" | custom-call | flops 8589934592 | bytes 8388608 | tf_op jit(solution)/shard_map/chol/pallas_call | solution.py:153
  236.3 2.6 add_bitcast_fusion
  238.9 38.7 %all_to_all.25 = f32[64,8,1024]{2,1,0:T(8,128)} all-to-all(f32[64,8,1024]{2,1,0:T(8,128)S(1)} %add_bitcast_fusion), channel_id=1, replica_groups=mesh['y'=4,'z'=4,'core'=2,'x'=4] {'y','z','x'}, dimensions={0} | all-to-all | bytes 4194304 | tf_op jit(solution)/shard_map/all_to_all | solution.py:456
  277.6 2.3 reduce_sum.38.y_ref
  280.0 1.6 copy-done.4
  281.6 7.1 %thin.2 = (f32[1024,1024]{1,0:T(8,128)}, f32[128,8,128]{2,1,0:T(8,128)}) custom-call(s32[5]{0:T(128)} %copy-done, f32[8,1024]{1,0:T(8,128)} %reduce_sum.38.y_ref, f32[5632,128]{1,0:T(8,128)} %chol.1.mine_ref, f32[5632,128]{1,0:T(8,128)} %copy-done.4), custom_call_target="tpu_custom_call" | custom-call | tf_op jit(solution)/shard_map/thin/pallas_call | solution.py:235
  288.6 20.7 %all_to_all.26 = f32[128,8,128]{2,1,0:T(8,128)} all-to-all(f32[128,8,128]{2,1,0:T(8,128)} %get-tuple-element.18), channel_id=1, replica_groups=mesh['y'=4,'z'=4,'core'=2,'x'=4] {'core','y','z','x'}, dimensions={0} | all-to-all | bytes 1048576 | tf_op jit(solution)/shard_map/all_to_all | solution.py:525
  309.4 6.4 %thin.3 = (f32[1024,1024]{1,0:T(8,128)}, f32[8,1024]{1,0:T(8,128)}) custom-call(s32[5]{0:T(128)} %copy-done, f32[1024,128]{1,0:T(8,128)} %bitcast.27, f32[5632,128]{1,0:T(8,128)} %chol.1.mine_ref, f32[5632,128]{1,0:T(8,128)} %copy-done.4), custom_call_target="tpu_custom_call" | custom-call | tf_op jit(solution)/shard_map/thin/pallas_call | solution.py:235
  (44 shorter events, 5.1 us)
Async XLA Ops:
  7.4 9.1 %all-to-all-start = ((s32[4,2,1024]{2,1,0:T(2,128)}), s32[4,2,1024]{2,1,0:T(2,128)S(1)}, u32[]{:S(2)}, u32[]{:S(2)}) async-start(s32[4,2,1024]{2,1,0:T(2,128)} %copy.10), calls=%async_computation | async-start | bytes 65536 | tf_op jit(solution)/shard_map/all_to_all | solution.py:500
  13.5 20.0 %copy-start = (s32[5]{0:T(128)}, s32[5]{0:T(128)S(1)}, u32[]{:S(2)}) copy-start(s32[5]{0:T(128)S(1)} %stack.28.core_ref) | copy-start | bytes 64
  16.6 16.9 %copy-start.8 = (s32[4,1,1024]{2,1,0:T(1,128)}, s32[4,1,1024]{2,1,0:T(1,128)S(1)}, u32[]{:S(2)}) copy-start(s32[4,1,1024]{2,1,0:T(1,128)S(1)} %get-tuple-element.23) | copy-start | bytes 49156
  17.9 2.2 copy-start.1
  20.1 1.6 copy-start.2
  33.4 6.3 %collective-permute-start.5 = (f32[4608,128]{1,0:T(8,128)S(1)}, f32[4608,128]{1,0:T(8,128)S(1)}, u32[]{:S(2)}, u32[]{:S(2)}) collective-permute-start(f32[4608,128]{1,0:T(8,128)S(1)} %get-tuple-element.16), channel_id=1, source_target_pairs={{0,4},{4,0},{1,5},{5,1},{2,6},{6,2},{3,7},{7,3},{8,12},{12,8},{9,1... | collective-permute-start | bytes 7077896 | tf_op jit(solution)/shard_map/ppermute | solution.py:446
  41.5 9.7 %copy-start.3 = (bf16[1024,1024]{1,0:T(8,128)(2,1)S(1)}, bf16[1024,1024]{1,0:T(8,128)(2,1)}, u32[]{:S(2)}) copy-start(bf16[1024,1024]{1,0:T(8,128)(2,1)} %u_ref.1) | copy-start | bytes 6291460
  41.5 84.8 %all-to-all-start.2 = ((f32[64,72,128]{2,1,0:T(8,128)}), f32[64,72,128]{2,1,0:T(8,128)}, u32[]{:S(2)}, u32[]{:S(2)}) async-start(f32[64,72,128]{2,1,0:T(8,128)} %bitcast.25), calls=%async_computation.2 | async-start | bytes 4718592 | tf_op jit(solution)/shard_map/all_to_all | solution.py:456
  51.2 71.0 %collective-permute-start.2 = (bf16[1024,1024]{1,0:T(8,128)(2,1)S(1)}, bf16[1024,1024]{1,0:T(8,128)(2,1)S(1)}, u32[]{:S(2)}, u32[]{:S(2)}) collective-permute-start(bf16[1024,1024]{1,0:T(8,128)(2,1)S(1)} %copy-done.3), channel_id=1, source_target_pairs={{0,3},{1,0},{2,1},{3,2},{4,7},{5,4},{6,5},{7,6},{8,11},{9,8},{10,9... | collective-permute-start | bytes 6291464 | tf_op jit(solution)/shard_map/ppermute | solution.py:468
  53.4 70.7 %collective-permute-start = (bf16[1024,1024]{1,0:T(8,128)(2,1)S(1)}, bf16[1024,1024]{1,0:T(8,128)(2,1)S(1)}, u32[]{:S(2)}, u32[]{:S(2)}) collective-permute-start(bf16[1024,1024]{1,0:T(8,128)(2,1)S(1)} %copy-done.3), channel_id=1, source_target_pairs={{0,1},{1,2},{2,3},{3,0},{4,5},{5,6},{6,7},{7,4},{8,9},{9,10},{10,1... | collective-permute-start | bytes 6291464 | tf_op jit(solution)/shard_map/ppermute | solution.py:468
  122.1 2.0 copy-start.6
  122.2 57.1 %collective-permute-start.3 = (bf16[512,1024]{1,0:T(8,128)(2,1)S(1)}, bf16[512,1024]{1,0:T(8,128)(2,1)}, u32[]{:S(2)}, u32[]{:S(2)}) collective-permute-start(bf16[512,1024]{1,0:T(8,128)(2,1)S(1)} %slice.24), channel_id=1, source_target_pairs={{0,3},{1,0},{2,1},{3,2},{4,7},{5,4},{6,5},{7,6},{8,11},{9,8},{10,9... | collective-permute-start | bytes 3145736 | tf_op jit(solution)/shard_map/ppermute | solution.py:468
  124.1 1.7 copy-start.7
  125.8 53.5 %collective-permute-start.1 = (bf16[512,1024]{1,0:T(8,128)(2,1)}, bf16[512,1024]{1,0:T(8,128)(2,1)}, u32[]{:S(2)}, u32[]{:S(2)}) collective-permute-start(bf16[512,1024]{1,0:T(8,128)(2,1)} %slice.23), channel_id=1, source_target_pairs={{0,1},{1,2},{2,3},{3,0},{4,5},{5,6},{6,7},{7,4},{8,9},{9,10},{10,1... | collective-permute-start | bytes 3145736 | tf_op jit(solution)/shard_map/ppermute | solution.py:468
  129.7 67.8 %all-to-all-start.3 = ((f32[64,72,128]{2,1,0:T(8,128)}), f32[64,72,128]{2,1,0:T(8,128)S(1)}, u32[]{:S(2)}, u32[]{:S(2)}) async-start(f32[64,72,128]{2,1,0:T(8,128)} %broadcast_in_dim.37), calls=%async_computation.3 | async-start | bytes 4718592 | tf_op jit(solution)/shard_map/all_to_all | solution.py:460
  195.1 41.1 %collective-permute-start.4 = (f32[512,1024]{1,0:T(8,128)}, f32[512,1024]{1,0:T(8,128)}, u32[]{:S(2)}, u32[]{:S(2)}) collective-permute-start(f32[512,1024]{1,0:T(8,128)} %get-tuple-element.14), channel_id=1, source_target_pairs={{0,4},{4,0},{1,5},{5,1},{2,6},{6,2},{3,7},{7,3},{8,12},{12,8},{9,1... | collective-permute-start | bytes 6291464 | tf_op jit(solution)/shard_map/ppermute | solution.py:446
  197.6 1.4 copy-start.5
  236.2 43.8 %collective-permute-start.6 = (f32[5632,128]{1,0:T(8,128)}, f32[5632,128]{1,0:T(8,128)S(1)}, u32[]{:S(2)}, u32[]{:S(2)}) collective-permute-start(f32[5632,128]{1,0:T(8,128)} %chol.1.mine_ref), channel_id=1, source_target_pairs={{0,4},{4,0},{1,5},{5,1},{2,6},{6,2},{3,7},{7,3},{8,12},{12,8},{9,1... | collective-permute-start | bytes 8650760 | tf_op jit(solution)/shard_map/ppermute | solution.py:446
  280.0 1.6 copy-start.4

commit v3 on v2

--- a/solution.py
+++ b/solution.py
@@ -250,15 +250,19 @@
     )(core, y, mine, other)
 
 
-def gram_kernel(core_ref, cu_ref, ci_ref, u_ref, i_ref, keep_ref, give_ref, counts, acc):
+def gram_kernel(core_ref, cu_ref, ci_ref, u_ref, i_ref, keep_ref, give_ref, counts, acc, u_buf, i_buf, packs, got, left):
     eye = lax.broadcasted_iota(jnp.int32, (NB, NB), 0) == lax.broadcasted_iota(jnp.int32, (NB, NB), 1)
 
-    def put(ref):
-        for i, j in PAIRS_OF:
-            at = START[i, j]
-            ref[at:at + NB, :] = acc[NB * i:NB * (i + 1), NB * j:NB * (j + 1)]
-
-    for maker, table in enumerate((u_ref, i_ref)):
+    def fetch(n):
+        return pltpu.make_async_copy((u_ref, i_ref)[n], (u_buf, i_buf)[n], got.at[n])
+
+    def leave(n, ref):
+        return pltpu.make_async_copy(packs.at[n], ref, left.at[n])
+
+    fetch(0).start()
+    fetch(1).start()
+    for maker, table in enumerate((u_buf, i_buf)):
+        fetch(maker).wait()
         rows = table.shape[0]
         counts[:rows // NB, :] = ci_ref[...] if maker else cu_ref[...]
         acc[...] = jnp.zeros((N, N), F32)
@@ -279,8 +283,13 @@
             return 0
 
         lax.fori_loop(0, 2, chunks, 0)
-        pl.when(core_ref[0] == maker)(lambda: put(keep_ref))
-        pl.when(core_ref[0] != maker)(lambda: put(give_ref))
+        for i, j in PAIRS_OF:
+            at = START[i, j]
+            packs[maker, at:at + NB, :] = acc[NB * i:NB * (i + 1), NB * j:NB * (j + 1)]
+        pl.when(core_ref[0] == maker)(lambda maker=maker: leave(maker, keep_ref).start())
+        pl.when(core_ref[0] != maker)(lambda maker=maker: leave(maker, give_ref).start())
+    for maker in range(2):
+        leave(maker, keep_ref).wait()
 
 
 def grams(core, user_counts, item_counts, user_table, item_table):
@@ -288,10 +297,18 @@
     return pl.pallas_call(
         gram_kernel,
         out_shape=(packed, packed),
-        in_specs=[SM, VM, VM, VM, VM],
-        out_specs=(VM, VM),
-        scratch_shapes=[pltpu.VMEM((16, NB), F32), pltpu.VMEM((N, N), F32)],
-        compiler_params=PARAMS,
+        in_specs=[SM, VM, VM, HBM, HBM],
+        out_specs=(HBM, HBM),
+        scratch_shapes=[
+            pltpu.VMEM((16, NB), F32),
+            pltpu.VMEM((N, N), F32),
+            pltpu.VMEM(user_table.shape, BF16),
+            pltpu.VMEM(item_table.shape, BF16),
+            pltpu.VMEM((2, PACKED, NB), F32),
+            pltpu.SemaphoreType.DMA((2,)),
+            pltpu.SemaphoreType.DMA((2,)),
+        ],
+        compiler_params=pltpu.CompilerParams(vmem_limit_bytes=60 << 20),
         cost_estimate=pl.CostEstimate(flops=1 << 33, bytes_accessed=10 << 20, transcendentals=0),
         name="grams",
     )(core, user_counts, item_counts, user_table, item_table)

time: 317 us -> 317 us (level)
  local copies, waits for them, and re-layouts: 11 us -> 7.73 us
    unnamed x18 -> x10, local copies, waits for them, and re-layouts: 7.36 us -> 3.6 us
    pallas_call x1, Pallas kernels: 11.7 us -> 14.9 us  [grams(): pl.pallas_call(gram_kernel, out_shape=(packed, packed), in_specs=[SM, VM,...]
where the time goes in v3:
time: 317 us; the launch traced here: 316 us
  Pallas kernels  122 us (38%)
  waiting for transfers between devices  75 us (24%)
  blocking collectives  59.4 us (19%)
  starting transfers between devices  32.7 us (10%)
  other arithmetic  15 us (5%)
  local copies, waits for them, and re-layouts  7.73 us (2%)
    ppermute x4, waiting for transfers between devices, shift(): return lax.ppermute(b, axis, ring(k % 4))  68.7 us
    pallas_call x3, Pallas kernels, cross(): pl.pallas_call(functools.partial(cross_kernel, groups=groups, first=first...  56.3 us
    all_to_all x1, blocking collectives, chip_scatter(): return jnp.sum(lax.all_to_all(b, CHIPS, 0, 0, tiled=True), 0)  38.7 us
    pallas_call x1, Pallas kernels, chol(): pl.pallas_call(functools.partial(chol_kernel, scale), out_shape=jax.Shape...  37.2 us
    all_to_all x1, blocking collectives, body(): left = lax.all_to_all(left, CORE_FIRST, 0, 0, tiled=True).reshape(width, NB)  20.7 us
    pallas_call x1, Pallas kernels, grams(): pl.pallas_call(gram_kernel, out_shape=(packed, packed), in_specs=[SM, VM,...  14.9 us
    pallas_call x2, Pallas kernels, thin(): pl.pallas_call(functools.partial(thin_kernel, maker=maker, scale=scale),...  13.5 us
    all_to_all x1, starting transfers between devices, chip_gather(): lax.all_to_all(jnp.broadcast_to(b[None], (64,) + b.shape), CHIPS, 0, 0, t...  9.59 us
  transfers between devices with their start and end apart: 10, of which 3 were waited for; matrix products, arithmetic and copies ran while one was open for 3% of the time, Pallas kernels for 30%

profile of v3, /device:TPU:1, one launch (start us, length us, event | category | flops | bytes accessed | tf_op | source)
XLA Modules:
  0.0 316.0 jit_solution(9526543690492381535)
XLA Ops:
  1.3 0.7 fusion.25
  2.5 0.8 add_select_fusion.5
  3.2 3.4 %select_reduce_fusion = s32[4096]{0:T(1024)S(1)} fusion(s32[2048]{0:T(1024)S(1)} %get-tuple-element.30, s32[2048]{0:T(1024)S(1)} %get-tuple-element.31), kind=kLoop, calls=%fused_computation | loop fusion | flops 25161728 | bytes 32768 | tf_op jit(solution)/shard_map/reduce_sum | solution.py:503
  7.4 4.8 %all-to-all-start = ((s32[4,2,1024]{2,1,0:T(2,128)}), s32[4,2,1024]{2,1,0:T(2,128)S(1)}, u32[]{:S(2)}, u32[]{:S(2)}) async-start(s32[4,2,1024]{2,1,0:T(2,128)} %copy.10), calls=%async_computation | async-start | bytes 65536 | tf_op jit(solution)/shard_map/all_to_all | solution.py:517
  12.2 0.7 fusion.26
  12.9 1.0 fusion.2.cu_ref
  14.6 1.9 all-to-all-done
  17.2 1.3 fusion.ci_ref
  18.5 14.9 %grams.1 = (f32[4608,128]{1,0:T(8,128)}, f32[4608,128]{1,0:T(8,128)}) custom-call(s32[5]{0:T(128)} %stack.28.core_ref, f32[8,128]{1,0:T(8,128)} %fusion.2.cu_ref, f32[16,128]{1,0:T(8,128)} %fusion.ci_ref, bf16[1024,1024]{1,0:T(8,128)(2,1)} %u_ref.1, bf16[2048,1024]{1,0:T(8,128)(2,1)} %i_ref.7), custom_call_target="tpu_custom_call" | custom-call | flops 8589934592 | bytes 10485760 | tf_op jit(solution)/shard_map/grams/pallas_call | solution.py:297
  33.5 2.2 collective-permute-start.5
  35.7 4.4 %collective-permute-done.5 = f32[4608,128]{1,0:T(8,128)S(1)} collective-permute-done((f32[4608,128]{1,0:T(8,128)}, f32[4608,128]{1,0:T(8,128)S(1)}, u32[]{:S(2)}, u32[]{:S(2)}) %collective-permute-start.5) | collective-permute-done | bytes 2359328 | tf_op jit(solution)/shard_map/ppermute | solution.py:463
  40.0 3.4 %add.129 = f32[4608,128]{1,0:T(8,128)} add(f32[4608,128]{1,0:T(8,128)} %get-tuple-element.15, f32[4608,128]{1,0:T(8,128)S(1)} %collective-permute-done.5) | non-fusion elementwise | flops 589824 | bytes 7077888 | tf_op jit(solution)/shard_map/add | solution.py:528
  43.5 9.3 %all-to-all-start.2 = ((f32[64,72,128]{2,1,0:T(8,128)}), f32[64,72,128]{2,1,0:T(8,128)S(1)}, u32[]{:S(2)}, u32[]{:S(2)}) async-start(f32[64,72,128]{2,1,0:T(8,128)} %bitcast.12), calls=%async_computation.2 | async-start | bytes 4718592 | tf_op jit(solution)/shard_map/all_to_all | solution.py:473
  52.7 2.5 collective-permute-start.2
  55.2 68.7 %collective-permute-done.2.refs_1_ = bf16[1024,1024]{1,0:T(8,128)(2,1)S(1)} collective-permute-done((bf16[1024,1024]{1,0:T(8,128)(2,1)}, bf16[1024,1024]{1,0:T(8,128)(2,1)S(1)}, u32[]{:S(2)}, u32[]{:S(2)}) %collective-permute-start.2) | collective-permute-done | bytes 2097184 | tf_op jit(solution)/shard_map/ppermute | solution.py:485
  124.0 1.9 collective-permute-start.3
  125.9 1.1 slice.23
  127.7 1.6 broadcast_in_dim.37
  129.3 9.6 %all-to-all-start.3 = ((f32[64,72,128]{2,1,0:T(8,128)}), f32[64,72,128]{2,1,0:T(8,128)S(1)}, u32[]{:S(2)}, u32[]{:S(2)}) async-start(f32[64,72,128]{2,1,0:T(8,128)} %broadcast_in_dim.37), calls=%async_computation.3 | async-start | bytes 4718592 | tf_op jit(solution)/shard_map/all_to_all | solution.py:477
  138.9 15.4 %cross.3.refs_2_ = f32[1024,1024]{1,0:T(8,128)} custom-call(s32[5]{0:T(128)} %stack.28.core_ref, s32[4096]{0:T(1024)} %get-tuple-element.27.at_ref, s32[4096]{0:T(1024)} %bitcast.29, bf16[2048,1024]{1,0:T(8,128)(2,1)} %i_ref.7, bf16[1024,1024]{1,0:T(8,128)(2,1)} %u_ref.1), custom_call_target="tpu_custom_call" | custom-call | flops 4294967296 | bytes 12582912 | tf_op jit(solution)/shard_map/cross/pallas_call | solution.py:432
  154.3 25.1 %cross.4.refs_2_ = f32[1024,1024]{1,0:T(8,128)} custom-call(s32[5]{0:T(128)} %stack.28.core_ref, s32[4096]{0:T(1024)} %get-tuple-element.27.at_ref, s32[4096]{0:T(1024)} %bitcast.30, bf16[2048,1024]{1,0:T(8,128)(2,1)} %i_ref.7, bf16[1024,1024]{1,0:T(8,128)(2,1)} %copy-done.3, bf16[1024,1024]{1,0:T(8,128)(2,1)} %copy-done.2, f32[1024,1024]{1,0:T(8,128)} %cross.3.refs_2_), custom_call_target="tpu_custom_call" | custom-call | flops 8589934592 | bytes 12582912 | tf_op jit(solution)/shard_map/cross/pallas_call | solution.py:432
  179.5 15.8 %cross.5 = (f32[512,1024]{1,0:T(8,128)}, f32[512,1024]{1,0:T(8,128)}) custom-call(s32[5]{0:T(128)} %stack.28.core_ref, s32[4096]{0:T(1024)} %get-tuple-element.27.at_ref, s32[4096]{0:T(1024)} %bitcast.31, bf16[2048,1024]{1,0:T(8,128)(2,1)} %i_ref.7, bf16[512,1024]{1,0:T(8,128)(2,1)} %collective-permute-done.1.refs_0_, ...), custom_call_target="tpu_custom_call" | custom-call | flops 4294967296 | bytes 12582912 | tf_op jit(solution)/shard_map/cross/pallas_call | solution.py:432
  195.3 2.4 collective-permute-start.4
  197.7 1.4 copy-done.1
  199.1 37.2 %chol.1.mine_ref = f32[5632,128]{1,0:T(8,128)} custom-call(f32[4608,128]{1,0:T(8,128)} %bitcast.25), custom_call_target="tpu_custom_call" | custom-call | flops 8589934592 | bytes 8388608 | tf_op jit(solution)/shard_map/chol/pallas_call | solution.py:153
  236.4 2.6 add_bitcast_fusion
  239.0 38.7 %all_to_all.25 = f32[64,8,1024]{2,1,0:T(8,128)} all-to-all(f32[64,8,1024]{2,1,0:T(8,128)S(1)} %add_bitcast_fusion), channel_id=1, replica_groups=mesh['y'=4,'z'=4,'core'=2,'x'=4] {'y','z','x'}, dimensions={0} | all-to-all | bytes 4194304 | tf_op jit(solution)/shard_map/all_to_all | solution.py:473
  277.7 2.3 reduce_sum.38.y_ref
  280.0 1.6 copy-done
  281.6 7.1 %thin.2 = (f32[1024,1024]{1,0:T(8,128)}, f32[128,8,128]{2,1,0:T(8,128)}) custom-call(s32[5]{0:T(128)} %stack.28.core_ref, f32[8,1024]{1,0:T(8,128)} %reduce_sum.38.y_ref, f32[5632,128]{1,0:T(8,128)} %chol.1.mine_ref, f32[5632,128]{1,0:T(8,128)} %copy-done), custom_call_target="tpu_custom_call" | custom-call | tf_op jit(solution)/shard_map/thin/pallas_call | solution.py:235
  288.7 20.7 %all_to_all.26 = f32[128,8,128]{2,1,0:T(8,128)} all-to-all(f32[128,8,128]{2,1,0:T(8,128)} %get-tuple-element.18), channel_id=1, replica_groups=mesh['y'=4,'z'=4,'core'=2,'x'=4] {'core','y','z','x'}, dimensions={0} | all-to-all | bytes 1048576 | tf_op jit(solution)/shard_map/all_to_all | solution.py:542
  309.4 6.4 %thin.3 = (f32[1024,1024]{1,0:T(8,128)}, f32[8,1024]{1,0:T(8,128)}) custom-call(s32[5]{0:T(128)} %stack.28.core_ref, f32[1024,128]{1,0:T(8,128)} %bitcast.26, f32[5632,128]{1,0:T(8,128)} %chol.1.mine_ref, f32[5632,128]{1,0:T(8,128)} %copy-done), custom_call_target="tpu_custom_call" | custom-call | tf_op jit(solution)/shard_map/thin/pallas_call | solution.py:235
  (36 shorter events, 3.4 us)
Async XLA Ops:
  7.4 9.1 %all-to-all-start = ((s32[4,2,1024]{2,1,0:T(2,128)}), s32[4,2,1024]{2,1,0:T(2,128)S(1)}, u32[]{:S(2)}, u32[]{:S(2)}) async-start(s32[4,2,1024]{2,1,0:T(2,128)} %copy.10), calls=%async_computation | async-start | bytes 65536 | tf_op jit(solution)/shard_map/all_to_all | solution.py:517
  16.6 16.9 %copy-start.4 = (s32[4,1,1024]{2,1,0:T(1,128)}, s32[4,1,1024]{2,1,0:T(1,128)S(1)}, u32[]{:S(2)}) copy-start(s32[4,1,1024]{2,1,0:T(1,128)S(1)} %get-tuple-element.23) | copy-start | bytes 49156
  33.5 6.6 %collective-permute-start.5 = (f32[4608,128]{1,0:T(8,128)}, f32[4608,128]{1,0:T(8,128)S(1)}, u32[]{:S(2)}, u32[]{:S(2)}) collective-permute-start(f32[4608,128]{1,0:T(8,128)} %get-tuple-element.16), channel_id=1, source_target_pairs={{0,4},{4,0},{1,5},{5,1},{2,6},{6,2},{3,7},{7,3},{8,12},{12,8},{9,1... | collective-permute-start | bytes 7077896 | tf_op jit(solution)/shard_map/ppermute | solution.py:463
  43.5 84.1 %all-to-all-start.2 = ((f32[64,72,128]{2,1,0:T(8,128)}), f32[64,72,128]{2,1,0:T(8,128)S(1)}, u32[]{:S(2)}, u32[]{:S(2)}) async-start(f32[64,72,128]{2,1,0:T(8,128)} %bitcast.12), calls=%async_computation.2 | async-start | bytes 4718592 | tf_op jit(solution)/shard_map/all_to_all | solution.py:473
  52.7 71.2 %collective-permute-start.2 = (bf16[1024,1024]{1,0:T(8,128)(2,1)}, bf16[1024,1024]{1,0:T(8,128)(2,1)S(1)}, u32[]{:S(2)}, u32[]{:S(2)}) collective-permute-start(bf16[1024,1024]{1,0:T(8,128)(2,1)} %u_ref.1), channel_id=1, source_target_pairs={{0,3},{1,0},{2,1},{3,2},{4,7},{5,4},{6,5},{7,6},{8,11},{9,8},{10,9... | collective-permute-start | bytes 6291464 | tf_op jit(solution)/shard_map/ppermute | solution.py:485
  55.2 70.7 %collective-permute-start = (bf16[1024,1024]{1,0:T(8,128)(2,1)}, bf16[1024,1024]{1,0:T(8,128)(2,1)S(1)}, u32[]{:S(2)}, u32[]{:S(2)}) collective-permute-start(bf16[1024,1024]{1,0:T(8,128)(2,1)} %u_ref.1), channel_id=1, source_target_pairs={{0,1},{1,2},{2,3},{3,0},{4,5},{5,6},{6,7},{7,4},{8,9},{9,10},{10,1... | collective-permute-start | bytes 6291464 | tf_op jit(solution)/shard_map/ppermute | solution.py:485
  123.9 3.1 copy-start.2
  124.0 55.5 %collective-permute-start.3 = (bf16[512,1024]{1,0:T(8,128)(2,1)S(1)}, bf16[512,1024]{1,0:T(8,128)(2,1)}, u32[]{:S(2)}, u32[]{:S(2)}) collective-permute-start(bf16[512,1024]{1,0:T(8,128)(2,1)S(1)} %slice.24), channel_id=1, source_target_pairs={{0,3},{1,0},{2,1},{3,2},{4,7},{5,4},{6,5},{7,6},{8,11},{9,8},{10,9... | collective-permute-start | bytes 3145736 | tf_op jit(solution)/shard_map/ppermute | solution.py:485
  125.9 1.7 copy-start.3
  127.6 51.9 %collective-permute-start.1 = (bf16[512,1024]{1,0:T(8,128)(2,1)}, bf16[512,1024]{1,0:T(8,128)(2,1)}, u32[]{:S(2)}, u32[]{:S(2)}) collective-permute-start(bf16[512,1024]{1,0:T(8,128)(2,1)} %slice.23), channel_id=1, source_target_pairs={{0,1},{1,2},{2,3},{3,0},{4,5},{5,6},{6,7},{7,4},{8,9},{9,10},{10,1... | collective-permute-start | bytes 3145736 | tf_op jit(solution)/shard_map/ppermute | solution.py:485
  129.3 68.4 %all-to-all-start.3 = ((f32[64,72,128]{2,1,0:T(8,128)}), f32[64,72,128]{2,1,0:T(8,128)S(1)}, u32[]{:S(2)}, u32[]{:S(2)}) async-start(f32[64,72,128]{2,1,0:T(8,128)} %broadcast_in_dim.37), calls=%async_computation.3 | async-start | bytes 4718592 | tf_op jit(solution)/shard_map/all_to_all | solution.py:477
  195.3 41.1 %collective-permute-start.4 = (f32[512,1024]{1,0:T(8,128)}, f32[512,1024]{1,0:T(8,128)}, u32[]{:S(2)}, u32[]{:S(2)}) collective-permute-start(f32[512,1024]{1,0:T(8,128)} %get-tuple-element.14), channel_id=1, source_target_pairs={{0,4},{4,0},{1,5},{5,1},{2,6},{6,2},{3,7},{7,3},{8,12},{12,8},{9,1... | collective-permute-start | bytes 6291464 | tf_op jit(solution)/shard_map/ppermute | solution.py:463
  197.7 1.4 copy-start.1
  236.3 43.8 %collective-permute-start.6 = (f32[5632,128]{1,0:T(8,128)}, f32[5632,128]{1,0:T(8,128)S(1)}, u32[]{:S(2)}, u32[]{:S(2)}) collective-permute-start(f32[5632,128]{1,0:T(8,128)} %chol.1.mine_ref), channel_id=1, source_target_pairs={{0,4},{4,0},{1,5},{5,1},{2,6},{6,2},{3,7},{7,3},{8,12},{12,8},{9,1... | collective-permute-start | bytes 8650760 | tf_op jit(solution)/shard_map/ppermute | solution.py:463
  280.0 1.6 copy-start
